TPU v7x, 32 devices: a whole 2x2x4 slice. The times are simulated.
32 devices in a mesh: dp: 16 (over z, y, x), mp: 2 (over core).
Axes of the slice: x: 2, y: 2, z: 4, core: 2. Of those that a mesh axis runs over, the one named last changes fastest.
Arguments:
- tokens: bfloat16 [24576, 768], P('dp', 'mp'), may hold values from -6 to 6
- norm1_gain: float32 [768], replicated, may hold values from 0.5 to 1.5
- norm1_bias: float32 [768], replicated, may hold values from -1.5 to 1.5
- qkv_weight: bfloat16 [768, 3, 768], P(None, None, 'mp'), may hold values from -0.21875 to 0.21875
- qv_bias: float32 [2, 768], P(None, 'mp'), may hold values from -2.5 to 2.5
- out_weight: bfloat16 [768, 768], P('mp'), may hold values from -2 to 2
- out_bias: float32 [768], replicated, may hold values from -1.5 to 1.5
- norm2_gain: float32 [768], replicated, may hold values from 0.5 to 1.5
- norm2_bias: float32 [768], replicated, may hold values from -1.5 to 1.5
- up_weight: bfloat16 [768, 3072], P(None, 'mp'), may hold values from -0.21875 to 0.21875
- up_bias: float32 [3072], P('mp'), may hold values from -2.5 to 2.5
- down_weight: bfloat16 [3072, 768], P('mp'), may hold values from -0.109375 to 0.109375
- down_bias: float32 [768], replicated, may hold values from -1.5 to 1.5
- out_grad: bfloat16 [24576, 768], P('dp', 'mp'), may hold values from -6 to 6
- send_slot: int32 [24576], P('dp'), may hold values from 0 to 3071, as said below
- pack_index: int32 [24576], P('dp'), may hold values from 0 to 3071, as said below
- clip_ids: int32 [24576], P('dp'), may hold values from 0 to 3, as said below
Outputs:
- out: bfloat16 [24576, 768], P('dp', 'mp')
- tokens_grad: bfloat16 [24576, 768], P('dp', 'mp')
- norm1_gain_grad: float32 [768], replicated
- norm1_bias_grad: float32 [768], replicated
- qkv_weight_grad: float32 [768, 3, 768], P('dp', None, 'mp')
- qv_bias_grad: float32 [2, 768], P(None, 'mp')
- out_weight_grad: float32 [768, 768], P('mp', 'dp')
- out_bias_grad: float32 [768], replicated
- norm2_gain_grad: float32 [768], replicated
- norm2_bias_grad: float32 [768], replicated
- up_weight_grad: float32 [768, 3072], P('dp', 'mp')
- up_bias_grad: float32 [3072], P('mp')
- down_weight_grad: float32 [3072, 768], P('mp', 'dp')
- down_bias_grad: float32 [768], replicated
Inputs may be any that keep to these rules, and one draw needn't show every extreme that they name: `send_slot`: on each index of dp the 1536 rows name distinct slots; slot // 192 is the group that receives the row. Each index sends exactly 192 rows to half of the groups and none to the others, and each group receives from exactly half of the indices. `pack_index`: arriving slot s = i * 192 + j of a group holds the row that index i of dp sent with slot (group * 192 + j); the 1536 packed rows of a group name distinct slots that all carry a row. `clip_ids`: never falling along a group's packed rows; rows attend only to rows of their group with the same number. Some group holds a clip of exactly 1190 rows.
All inputs are finite; a program needn't handle non-finite values.
Results may differ from a plain program's by a relative error of at most 0.018.
Values may be sent and summed in bfloat16 or wider, within the bound.
No kernel may reach another device: no remote copies, remote signals or barrier semaphores. Data moves between devices by JAX's collectives and lax.ppermute only.
A program may use at most 256 MiB of HBM per device.

v0:
```python
import jax
import jax.numpy as jnp
from jax import lax
from jax.sharding import PartitionSpec as P

HEAD_DIM = 64


NORM_EPS = 1e-06
MASK_FILL = -1e30


def norm_rows(values, gain_vec, shift_vec):
    center = values - jnp.mean(values, axis=-1, keepdims=True)
    spread = jnp.mean(center * center, axis=-1, keepdims=True)
    return center * lax.rsqrt(spread + NORM_EPS) * gain_vec + shift_vec


def gelu_exact(values):
    return jax.nn.gelu(values, approximate=False)


def masked_scores(query_block, key_rows, clip_block, clip_all, score_scale):
    raw_scores = (
        jnp.einsum("qhd,khd->hqk", query_block, key_rows, preferred_element_type=jnp.float32)
        * score_scale
    )
    same_clip = clip_block[:, None] == clip_all[None, :]
    return jnp.where(same_clip[None], raw_scores, MASK_FILL)


def local(
    tokens,
    norm1_gain,
    norm1_bias,
    qkv_weight,
    qv_bias,
    out_weight,
    out_bias,
    norm2_gain,
    norm2_bias,
    up_weight,
    up_bias,
    down_weight,
    down_bias,
    out_grad,
    send_slot,
    pack_index,
    clip_ids,
):
    row_count = tokens.shape[0]
    half_width = tokens.shape[1]
    slot_count = 2 * row_count
    mp_index = lax.axis_index("mp")
    head_count = half_width // HEAD_DIM
    score_scale = HEAD_DIM ** (-0.5)
    send_rows = jnp.zeros((slot_count, half_width), jnp.bfloat16).at[send_slot].set(tokens)
    send_grads = jnp.zeros((slot_count, half_width), jnp.bfloat16).at[send_slot].set(out_grad)
    recv_rows, recv_grads = (
        lax.all_to_all(send_rows, "dp", split_axis=0, concat_axis=0, tiled=True),
        lax.all_to_all(send_grads, "dp", split_axis=0, concat_axis=0, tiled=True),
    )
    full_rows, full_grads = (
        lax.all_gather(recv_rows[pack_index], "mp", axis=1, tiled=True),
        lax.all_gather(recv_grads[pack_index], "mp", axis=1, tiled=True),
    )
    inputs = full_rows.astype(jnp.float32)
    normed_f, norm1_pull = jax.vjp(norm_rows, inputs, norm1_gain, norm1_bias)
    normed = normed_f.astype(jnp.bfloat16)
    projected = jnp.einsum("rd,dtc->rtc", normed, qkv_weight, preferred_element_type=jnp.float32)
    query_rows = (
        (projected[:, 0] + qv_bias[0]).astype(jnp.bfloat16).reshape(row_count, head_count, HEAD_DIM)
    )
    key_rows = projected[:, 1].astype(jnp.bfloat16).reshape(row_count, head_count, HEAD_DIM)
    value_rows = (
        (projected[:, 2] + qv_bias[1]).astype(jnp.bfloat16).reshape(row_count, head_count, HEAD_DIM)
    )
    block_rows = min(512, row_count)
    block_count = row_count // block_rows

    def attend(block_index):
        start = block_index * block_rows
        query_block = lax.dynamic_slice_in_dim(query_rows, start, block_rows, 0)
        clip_block = lax.dynamic_slice_in_dim(clip_ids, start, block_rows, 0)
        scores = masked_scores(query_block, key_rows, clip_block, clip_ids, score_scale)
        row_max = jnp.max(scores, axis=-1, keepdims=True)
        exponent = jnp.exp(scores - row_max)
        row_total = jnp.sum(exponent, axis=-1, keepdims=True)
        probs_low = (exponent / row_total).astype(jnp.bfloat16)
        mixed_block = jnp.einsum(
            "hqk,khd->qhd", probs_low, value_rows, preferred_element_type=jnp.float32
        )
        return (mixed_block.astype(jnp.bfloat16), (row_max + jnp.log(row_total))[..., 0])

    mixed_blocks, log_totals = lax.map(attend, jnp.arange(block_count))
    mixed = mixed_blocks.reshape(row_count, half_width)
    attn_terms = jnp.dot(mixed, out_weight, preferred_element_type=jnp.float32)
    middle = inputs + lax.psum(attn_terms.astype(jnp.bfloat16), "mp").astype(jnp.float32) + out_bias
    normed_two_f, norm2_pull = jax.vjp(norm_rows, middle, norm2_gain, norm2_bias)
    normed_two = normed_two_f.astype(jnp.bfloat16)
    hidden_pre = jnp.dot(normed_two, up_weight, preferred_element_type=jnp.float32) + up_bias
    hidden_f, gelu_pull = jax.vjp(gelu_exact, hidden_pre)
    hidden = hidden_f.astype(jnp.bfloat16)
    down_terms = jnp.dot(hidden, down_weight, preferred_element_type=jnp.float32)
    down_half = lax.psum_scatter(
        down_terms.astype(jnp.bfloat16), "mp", scatter_dimension=1, tiled=True
    ).astype(jnp.float32)
    middle_half = lax.dynamic_slice_in_dim(middle, mp_index * half_width, half_width, 1)
    bias_half = lax.dynamic_slice_in_dim(down_bias, mp_index * half_width, half_width, 0)
    result_rows = (middle_half + down_half + bias_half).astype(jnp.bfloat16)
    result_slots = jnp.zeros((slot_count, half_width), jnp.bfloat16).at[pack_index].set(result_rows)
    out = lax.all_to_all(result_slots, "dp", split_axis=0, concat_axis=0, tiled=True)[send_slot]
    grads_f = full_grads.astype(jnp.float32)
    down_bias_grad = jnp.sum(grads_f, axis=0)
    down_weight_grad = jnp.einsum(
        "rf,rd->fd", hidden, full_grads, preferred_element_type=jnp.float32
    )
    hidden_grad = jnp.einsum(
        "rd,fd->rf", full_grads, down_weight, preferred_element_type=jnp.float32
    )
    (pre_grad_f,) = gelu_pull(hidden_grad)
    pre_grad = pre_grad_f.astype(jnp.bfloat16)
    up_bias_grad = jnp.sum(pre_grad.astype(jnp.float32), axis=0)
    up_weight_grad = jnp.einsum(
        "rd,rf->df", normed_two, pre_grad, preferred_element_type=jnp.float32
    )
    normed_two_terms = jnp.einsum(
        "rf,df->rd", pre_grad, up_weight, preferred_element_type=jnp.float32
    )
    normed_two_grad = lax.psum(normed_two_terms.astype(jnp.bfloat16), "mp").astype(jnp.float32)
    middle_norm_grad, norm2_gain_grad, norm2_bias_grad = norm2_pull(normed_two_grad)
    middle_grad = grads_f + middle_norm_grad
    out_bias_grad = jnp.sum(middle_grad, axis=0)
    middle_low = middle_grad.astype(jnp.bfloat16)
    out_weight_grad = jnp.einsum("rc,rd->cd", mixed, middle_low, preferred_element_type=jnp.float32)
    mixed_grad = jnp.einsum(
        "rd,cd->rc", middle_low, out_weight, preferred_element_type=jnp.float32
    ).astype(jnp.bfloat16)
    mixed_grad = mixed_grad.reshape(row_count, head_count, HEAD_DIM)

    def attend_back(carried, block_index):
        key_acc, value_acc = carried
        start = block_index * block_rows
        query_block = lax.dynamic_slice_in_dim(query_rows, start, block_rows, 0)
        clip_block = lax.dynamic_slice_in_dim(clip_ids, start, block_rows, 0)
        grad_block = lax.dynamic_slice_in_dim(mixed_grad, start, block_rows, 0)
        scores = masked_scores(query_block, key_rows, clip_block, clip_ids, score_scale)
        probs = jnp.exp(scores - log_totals[block_index][..., None])
        probs_low = probs.astype(jnp.bfloat16)
        prob_grad = jnp.einsum(
            "qhd,khd->hqk", grad_block, value_rows, preferred_element_type=jnp.float32
        )
        inner_sum = jnp.sum(prob_grad * probs, axis=-1, keepdims=True)
        score_grad = (probs * (prob_grad - inner_sum)).astype(jnp.bfloat16)
        query_grad = (
            jnp.einsum("hqk,khd->qhd", score_grad, key_rows, preferred_element_type=jnp.float32)
            * score_scale
        )
        key_acc = (
            key_acc
            + jnp.einsum(
                "hqk,qhd->khd", score_grad, query_block, preferred_element_type=jnp.float32
            )
            * score_scale
        )
        value_acc = value_acc + jnp.einsum(
            "hqk,qhd->khd", probs_low, grad_block, preferred_element_type=jnp.float32
        )
        return ((key_acc, value_acc), query_grad.astype(jnp.bfloat16))

    zero_heads = jnp.zeros((row_count, head_count, HEAD_DIM), jnp.float32)
    (key_total, value_total), query_blocks = lax.scan(
        attend_back, (zero_heads, zero_heads), jnp.arange(block_count)
    )
    query_grad = query_blocks.reshape(row_count, half_width)
    key_grad = key_total.astype(jnp.bfloat16).reshape(row_count, half_width)
    value_grad = value_total.astype(jnp.bfloat16).reshape(row_count, half_width)
    qv_bias_grad = jnp.stack(
        [
            jnp.sum(query_grad.astype(jnp.float32), axis=0),
            jnp.sum(value_grad.astype(jnp.float32), axis=0),
        ]
    )
    projected_grad = jnp.stack([query_grad, key_grad, value_grad], axis=1)
    qkv_weight_grad = jnp.einsum(
        "rd,rtc->dtc", normed, projected_grad, preferred_element_type=jnp.float32
    )
    normed_terms = jnp.einsum(
        "rtc,dtc->rd", projected_grad, qkv_weight, preferred_element_type=jnp.float32
    )
    normed_grad = lax.psum(normed_terms.astype(jnp.bfloat16), "mp").astype(jnp.float32)
    input_norm_grad, norm1_gain_grad, norm1_bias_grad = norm1_pull(normed_grad)
    input_grad = middle_grad + input_norm_grad
    input_half = lax.dynamic_slice_in_dim(input_grad, mp_index * half_width, half_width, 1).astype(
        jnp.bfloat16
    )
    input_slots = jnp.zeros((slot_count, half_width), jnp.bfloat16).at[pack_index].set(input_half)
    tokens_grad = lax.all_to_all(input_slots, "dp", split_axis=0, concat_axis=0, tiled=True)[
        send_slot
    ]
    qkv_weight_grad, out_weight_grad, up_weight_grad, down_weight_grad = (
        lax.psum_scatter(qkv_weight_grad, "dp", scatter_dimension=0, tiled=True),
        lax.psum_scatter(out_weight_grad, "dp", scatter_dimension=1, tiled=True),
        lax.psum_scatter(up_weight_grad, "dp", scatter_dimension=0, tiled=True),
        lax.psum_scatter(down_weight_grad, "dp", scatter_dimension=1, tiled=True),
    )
    (
        norm1_gain_grad,
        norm1_bias_grad,
        qv_bias_grad,
        out_bias_grad,
        norm2_gain_grad,
        norm2_bias_grad,
        up_bias_grad,
        down_bias_grad,
    ) = lax.psum(
        (
            norm1_gain_grad,
            norm1_bias_grad,
            qv_bias_grad,
            out_bias_grad,
            norm2_gain_grad,
            norm2_bias_grad,
            up_bias_grad,
            down_bias_grad,
        ),
        "dp",
    )
    return (
        out,
        tokens_grad,
        norm1_gain_grad,
        norm1_bias_grad,
        qkv_weight_grad,
        qv_bias_grad,
        out_weight_grad,
        out_bias_grad,
        norm2_gain_grad,
        norm2_bias_grad,
        up_weight_grad,
        up_bias_grad,
        down_weight_grad,
        down_bias_grad,
    )


def solution(mesh):
    in_specs = (
        P("dp", "mp"),
        P(),
        P(),
        P(None, None, "mp"),
        P(None, "mp"),
        P("mp", None),
        P(),
        P(),
        P(),
        P(None, "mp"),
        P("mp"),
        P("mp", None),
        P(),
        P("dp", "mp"),
        P("dp"),
        P("dp"),
        P("dp"),
    )
    out_specs = (
        P("dp", "mp"),
        P("dp", "mp"),
        P(),
        P(),
        P("dp", None, "mp"),
        P(None, "mp"),
        P("mp", "dp"),
        P(),
        P(),
        P(),
        P("dp", "mp"),
        P("mp"),
        P("mp", "dp"),
        P(),
    )
    return jax.shard_map(local, mesh=mesh, in_specs=in_specs, out_specs=out_specs, check_vma=False)
```

profile of v0, /device:TPU:0, one launch (start us, length us, event | category | flops | bytes accessed | tf_op | source)
XLA Modules:
  0.0 1127.9 jit_solution(16446879605268196734)
XLA Ops:
  8.1 9.4 scatter_custom_fusion
  17.4 8.4 all-to-all-start
  25.9 47.5 %all-to-all-done = bf16[16,192,384]{2,1,0:T(8,128)(2,1)} async-done(((bf16[16,192,384]{2,1,0:T(8,128)(2,1)}), bf16[16,192,384]{2,1,0:T(8,128)(2,1)}, u32[]{:S(2)}, u32[]{:S(2)}) %all-to-all-start) | async-done | bytes 2359328 | tf_op jit(solution)/shard_map/all_to_all | solution.py:60
  73.4 7.0 gather_fusion
  80.5 9.4 scatter_custom_fusion.2
  89.8 11.3 %all-to-all-start.2 = ((bf16[16,192,384]{2,1,0:T(8,128)(2,1)}), bf16[16,192,384]{2,1,0:T(8,128)(2,1)}, u32[]{:S(2)}, u32[]{:S(2)}) async-start(bf16[16,192,384]{2,1,0:T(8,128)(2,1)} %bitcast.114), calls=%async_computation.2 | async-start | bytes 4718592 | tf_op jit(solution)/shard_map/all_to_all | solution.py:61
  114.7 59.3 %while.27 = (s32[]{:T(128)}, bf16[3,512,6,64]{1,3,2,0:T(8,128)(2,1)}, f32[3,6,512]{2,1,0:T(8,128)}, s32[3]{0:T(128)S(1)}, s32[1536]{0:T(1024)S(1)}, /*index=5*/b...) while((s32[]{:T(128)}, ...), condition=%wide.region_6.7_spmd, body=%wide.region_3.6_spmd.sunk | while | flops 1265562624 | bytes 66175204 | solution.py:95
  116.7 4.8 fusion.136
  121.5 4.9 fusion.137
  126.3 7.6 fusion.138
  136.4 4.8 fusion.136
  141.2 4.9 fusion.137
  146.0 7.6 fusion.138
  156.1 4.8 fusion.136
  160.9 4.9 fusion.137
  165.7 7.6 fusion.138
  180.7 7.0 gather_fusion.2
  187.7 16.1 %all-reduce.5.cloned.1.call-done = bf16[1536,768]{1,0:T(8,128)(2,1)} async-done(((bf16[1536,768]{1,0:T(8,128)(2,1)}), bf16[1536,768]{1,0:T(8,128)(2,1)}) %all-reduce.5.cloned.1.call-update) | async-done | bytes 2359312 | tf_op jit(solution)/shard_map/psum | solution.py:98
  209.8 26.3 %multiply_convert_fusion.1 = (bf16[1536,1536]{1,0:T(8,128)(2,1)}, f32[1536,1536]{1,0:T(8,128)}, f32[1536,1536]{1,0:T(8,128)}) fusion(f32[1536]{0:T(1024)S(1)} %copy-done.47, bf16[768,1536]{1,0:T(8,128)(2,1)S(1)} %copy-done, f32[1536,768]{1,0:T(8,128)S(1)} %get-tuple-element.221, f32[768]{0:T(1024)S(1)} %copy-done.48, f32[768]{0:T(1024)S(1)} %copy-done.35, ...), kind=kOutput, calls=%fused_computation.57 | convolution fusion | flops 3785490432 | bytes 30695424 | tf_op jit(solution)/shard_map/dot_general | solution.py:101
  236.0 13.4 %convert_reduce_fusion = (f32[1536]{0:T(1024)}, bf16[1536,1536]{1,0:T(8,128)(2,1)S(1)}) fusion(f32[1536,1536]{1,0:T(8,128)} %get-tuple-element.219, f32[1536,1536]{1,0:T(8,128)} %get-tuple-element.229, bf16[1536,768]{1,0:T(8,128)(2,1)} %all-gather.7.cloned.1.call-done, bf16[1536,768]{1,0:T(8,128)(2,1)} %param.32), kind=kOutput, calls=%fused_computation.55 | convolution fusion | flops 3661625856 | bytes 28317696 | tf_op jit(solution)/shard_map/rd,fd->rf/dot_general | solution.py:118
  251.5 5.1 convolution_convert_fusion
  256.7 23.0 %all-reduce.7.cloned.1.call-done = bf16[1536,768]{1,0:T(8,128)(2,1)} async-done(((bf16[1536,768]{1,0:T(8,128)(2,1)}), bf16[1536,768]{1,0:T(8,128)(2,1)}) %all-reduce.7.cloned.1.call-update) | async-done | bytes 2359312 | tf_op jit(solution)/shard_map/psum | solution.py:130
  279.7 5.3 convert_reduce_fusion.2
  285.9 5.3 fusion.58
  291.3 5.0 fusion.86
  301.7 174.7 %while.28 = (s32[]{:T(128)}, f32[1536,6,64]{0,2,1:T(8,128)}, f32[1536,6,64]{0,2,1:T(8,128)}, bf16[3,512,6,64]{1,3,2,0:T(8,128)(2,1)}, s32[3]{0:T(128)S(1)}, /*in...) while((s32[]{:T(128)}, f32[1536,6,64]{0,2,1:T(8,128)}, ...), condition=%wide.region_18.19_spmd.clone, body=%wide.region_16.18_spmd.clone.sunk | while | flops 3094803456 | bytes 254116176 | solution.py:172
  306.6 3.6 fusion.148
  310.3 6.5 copy-done.2
  316.7 7.7 fusion.150
  324.4 14.1 %multiply_reduce_fusion.3 = (f32[6,512]{1,0:T(8,128)S(1)}, f32[6,512,1536]{2,1,0:T(8,128)}) fusion(f32[6,512,1536]{2,1,0:T(8,128)} %copy-done.2, f32[6,512]{1,0:T(8,128)S(1)} %dynamic-slice_bitcast_fusion.2, pred[512,1536]{1,0:T(8,128)(4,1)S(1)} %broadcast_compare_fusion.5, bf16[1536,6,64]{0,2,1:T(8,128)(2,1)} %get-tuple-element.436, ...), kind=kOutput, calls=%fused_computation.25.clone.1 | convolution fusion | flops 627569664 | bytes 40132612 | tf_op jit(solution)/shard_map/while/body/eval_jaxpr/qhd,khd->hqk/dot_general | solution.py:150
  338.6 13.2 %multiply_convert_fusion.3 = bf16[6,512,1536]{2,1,0:T(8,128)(2,1)S(1)} fusion(f32[6,512,1536]{2,1,0:T(8,128)} %get-tuple-element.356, f32[6,512,1536]{2,1,0:T(8,128)} %copy-done.2, f32[6,512]{1,0:T(8,128)S(1)} %get-tuple-element.357, f32[6,512]{1,0:T(8,128)S(1)} %dynamic-slice_bitcast_fusion.2, pred[512,1536]{1,0:T(8,128)(4,1)S(1)} %broadcast_compare_fusion.5), kind=kLoop, calls=%fused_computation.24.clone.1 | loop fusion | flops 28311552 | bytes 47996928 | tf_op jit(solution)/shard_map/while/body/eval_jaxpr/convert_element_type | solution.py:154
  351.8 3.7 fusion.151
  364.4 3.6 fusion.148
  368.0 6.5 copy-done.2
  374.5 8.2 fusion.150
  382.7 14.1 %multiply_reduce_fusion.3 = (f32[6,512]{1,0:T(8,128)S(1)}, f32[6,512,1536]{2,1,0:T(8,128)}) fusion(f32[6,512,1536]{2,1,0:T(8,128)} %copy-done.2, f32[6,512]{1,0:T(8,128)S(1)} %dynamic-slice_bitcast_fusion.2, pred[512,1536]{1,0:T(8,128)(4,1)S(1)} %broadcast_compare_fusion.5, bf16[1536,6,64]{0,2,1:T(8,128)(2,1)} %get-tuple-element.436, ...), kind=kOutput, calls=%fused_computation.25.clone.1 | convolution fusion | flops 627569664 | bytes 40132612 | tf_op jit(solution)/shard_map/while/body/eval_jaxpr/qhd,khd->hqk/dot_general | solution.py:150
  396.8 13.2 %multiply_convert_fusion.3 = bf16[6,512,1536]{2,1,0:T(8,128)(2,1)S(1)} fusion(f32[6,512,1536]{2,1,0:T(8,128)} %get-tuple-element.356, f32[6,512,1536]{2,1,0:T(8,128)} %copy-done.2, f32[6,512]{1,0:T(8,128)S(1)} %get-tuple-element.357, f32[6,512]{1,0:T(8,128)S(1)} %dynamic-slice_bitcast_fusion.2, pred[512,1536]{1,0:T(8,128)(4,1)S(1)} %broadcast_compare_fusion.5), kind=kLoop, calls=%fused_computation.24.clone.1 | loop fusion | flops 28311552 | bytes 47996928 | tf_op jit(solution)/shard_map/while/body/eval_jaxpr/convert_element_type | solution.py:154
  410.0 3.7 fusion.151
  422.6 3.6 fusion.148
  426.2 6.5 copy-done.2
  432.7 8.2 fusion.150
  440.9 14.1 %multiply_reduce_fusion.3 = (f32[6,512]{1,0:T(8,128)S(1)}, f32[6,512,1536]{2,1,0:T(8,128)}) fusion(f32[6,512,1536]{2,1,0:T(8,128)} %copy-done.2, f32[6,512]{1,0:T(8,128)S(1)} %dynamic-slice_bitcast_fusion.2, pred[512,1536]{1,0:T(8,128)(4,1)S(1)} %broadcast_compare_fusion.5, bf16[1536,6,64]{0,2,1:T(8,128)(2,1)} %get-tuple-element.436, ...), kind=kOutput, calls=%fused_computation.25.clone.1 | convolution fusion | flops 627569664 | bytes 40132612 | tf_op jit(solution)/shard_map/while/body/eval_jaxpr/qhd,khd->hqk/dot_general | solution.py:150
  455.0 13.2 %multiply_convert_fusion.3 = bf16[6,512,1536]{2,1,0:T(8,128)(2,1)S(1)} fusion(f32[6,512,1536]{2,1,0:T(8,128)} %get-tuple-element.356, f32[6,512,1536]{2,1,0:T(8,128)} %copy-done.2, f32[6,512]{1,0:T(8,128)S(1)} %get-tuple-element.357, f32[6,512]{1,0:T(8,128)S(1)} %dynamic-slice_bitcast_fusion.2, pred[512,1536]{1,0:T(8,128)(4,1)S(1)} %broadcast_compare_fusion.5), kind=kLoop, calls=%fused_computation.24.clone.1 | loop fusion | flops 28311552 | bytes 47996928 | tf_op jit(solution)/shard_map/while/body/eval_jaxpr/convert_element_type | solution.py:154
  468.3 3.7 fusion.151
  482.0 3.6 copy.52
  488.5 7.2 bitcast_convert_fusion
  495.8 6.9 convolution_convert_fusion.1
  505.4 5.1 fusion.67
  510.8 10.3 fusion.85
  523.1 7.1 fusion.62
  530.6 9.4 fusion.92
  540.6 4.3 fusion.59
  545.0 3.6 fusion.87
  548.6 10.1 scatter_custom_fusion.3
  558.7 7.1 all-to-all-start.3
  568.3 9.5 scatter_custom_fusion.1
  577.8 38.5 %all-to-all-done.3 = bf16[16,192,384]{2,1,0:T(8,128)(2,1)S(1)} async-done(((bf16[16,192,384]{2,1,0:T(8,128)(2,1)}), bf16[16,192,384]{2,1,0:T(8,128)(2,1)S(1)}, u32[]{:S(2)}, u32[]{:S(2)}) %all-to-all-start.3) | async-done | bytes 2359328 | tf_op jit(solution)/shard_map/all_to_all | solution.py:198
  616.3 11.9 %all-to-all-start.1 = ((bf16[16,192,384]{2,1,0:T(8,128)(2,1)}), bf16[16,192,384]{2,1,0:T(8,128)(2,1)}, u32[]{:S(2)}, u32[]{:S(2)}) async-start(bf16[16,192,384]{2,1,0:T(8,128)(2,1)} %bitcast.116), calls=%async_computation.1 | async-start | bytes 4718592 | tf_op jit(solution)/shard_map/all_to_all | solution.py:112
  629.3 111.3 %all-reduce = (f32[768]{0:T(1024)}, f32[768]{0:T(1024)}, f32[2,384]{1,0:T(2,128)}, f32[768]{0:T(1024)}, f32[768]{0:T(1024)}, /*index=5*/f32[768]{0:T(1024)}, f32[1536]{0:T(1024)}, f32[768]{0:T(1024)}) all-reduce(f32[768]{0:T(1024)} %get-tuple-element.159, f32[768]{0:T(1024)} %get-tuple-element.163, ...), channel_id=1, replica_groups=mesh['dp'=16,'mp'=2] {'dp'}, use_global_device_ids=true, to_apply=%region_24.25 | all-reduce | flops 6912 | bytes 55296 | tf_op jit(solution)/shard_map/psum | solution.py:216
  740.6 5.3 gather_fusion.3
  745.9 7.1 gather_fusion.1
  753.0 85.1 %reduce-scatter.12.cloned.1.call-done = f32[48,1536]{1,0:T(8,128)} async-done(((f32[768,1536]{1,0:T(8,128)}), f32[48,1536]{1,0:T(8,128)}) %reduce-scatter.12.cloned.1.call-update) | async-done | bytes 294928 | tf_op jit(solution)/shard_map/reduce_scatter | solution.py:204
  838.2 139.4 %reduce-scatter.8.cloned.1.call-done = f32[48,3,384]{2,0,1:T(8,128)} async-done(((f32[768,3,384]{2,0,1:T(8,128)}), f32[48,3,384]{2,0,1:T(8,128)}) %reduce-scatter.8.cloned.1.call-update) | async-done | bytes 221200 | tf_op jit(solution)/shard_map/reduce_scatter | solution.py:202
  977.6 143.1 %reduce-scatter.14.cloned.1.call-done = f32[1536,48]{0,1:T(8,128)} async-done(((f32[1536,768]{0,1:T(8,128)}), f32[1536,48]{0,1:T(8,128)}) %reduce-scatter.14.cloned.1.call-update) | async-done | bytes 294928 | tf_op jit(solution)/shard_map/reduce_scatter | solution.py:205
  (217 shorter events, 77.4 us)
Async XLA Ops:
  7.2 202.6 %copy-start = (bf16[768,1536]{1,0:T(8,128)(2,1)S(1)}, bf16[768,1536]{1,0:T(8,128)(2,1)}, u32[]{:S(2)}) copy-start(bf16[768,1536]{1,0:T(8,128)(2,1)} %param.30) | copy-start | bytes 7077892
  7.2 18.7 %copy-start.43 = (s32[1536]{0:T(1024)S(1)}, s32[1536]{0:T(1024)}, u32[]{:S(2)}) copy-start(s32[1536]{0:T(1024)} %param.36) | copy-start | bytes 18436
  8.1 72.4 %copy-start.38 = (s32[1536]{0:T(1024)}, s32[1536]{0:T(1024)S(1)}, u32[]{:S(2)}) copy-start(s32[1536]{0:T(1024)S(1)} %compare_select_fusion) | copy-start | bytes 18436
  17.4 56.0 %all-to-all-start = ((bf16[16,192,384]{2,1,0:T(8,128)(2,1)}), bf16[16,192,384]{2,1,0:T(8,128)(2,1)}, u32[]{:S(2)}, u32[]{:S(2)}) async-start(bf16[16,192,384]{2,1,0:T(8,128)(2,1)} %bitcast.117), calls=%async_computation | async-start | bytes 4718592 | tf_op jit(solution)/shard_map/all_to_all | solution.py:60
  25.8 76.1 %all-gather.5.cloned.1.call-start = ((), (), s32[]{:S(2)}) async-start(), calls=%async_computation.16 | async-start | bytes 3538944 | tf_op jit(solution)/shard_map/all_gather | solution.py:64
  25.9 54.5 %copy-start.40 = (s32[1536]{0:T(1024)}, s32[1536]{0:T(1024)S(1)}, u32[]{:S(2)}) copy-start(s32[1536]{0:T(1024)S(1)} %compare_select_fusion.1) | copy-start | bytes 18436
  25.9 54.5 %copy-start.28 = (s32[2048]{0:T(1024)}, s32[2048]{0:T(1024)S(1)}, u32[]{:S(2)}) copy-start(s32[2048]{0:T(1024)S(1)} %pad_clamp_fusion.1) | copy-start | bytes 24580
  80.4 21.3 %copy-start.44 = (f32[2,384]{1,0:T(2,128)S(1)}, f32[2,384]{1,0:T(2,128)}, u32[]{:S(2)}) copy-start(f32[2,384]{1,0:T(2,128)} %param.25) | copy-start | bytes 9220
  89.8 18.0 %copy-start.41 = (f32[768]{0:T(1024)S(1)}, f32[768]{0:T(1024)}, u32[]{:S(2)}) copy-start(f32[768]{0:T(1024)} %param.22) | copy-start | bytes 9220
  89.8 18.0 %copy-start.50 = (f32[768]{0:T(1024)S(1)}, f32[768]{0:T(1024)}, u32[]{:S(2)}) copy-start(f32[768]{0:T(1024)} %param.23) | copy-start | bytes 9220
  89.8 90.8 %all-to-all-start.2 = ((bf16[16,192,384]{2,1,0:T(8,128)(2,1)}), bf16[16,192,384]{2,1,0:T(8,128)(2,1)}, u32[]{:S(2)}, u32[]{:S(2)}) async-start(bf16[16,192,384]{2,1,0:T(8,128)(2,1)} %bitcast.114), calls=%async_computation.2 | async-start | bytes 4718592 | tf_op jit(solution)/shard_map/all_to_all | solution.py:61
  101.1 102.6 %all-reduce.5.cloned.1.call-start = ((), (), s32[]{:S(2)}) async-start(), calls=%async_computation.9 | async-start | bytes 4718592 | tf_op jit(solution)/shard_map/psum | solution.py:98
  101.9 5.9 copy-start.7
  101.9 5.9 copy-start.46
  104.1 2.5 copy-start.23
  111.8 2.9 copy-start.17
  116.7 4.8 copy-start.3
  136.4 4.8 copy-start.3
  156.1 4.8 copy-start.3
  173.9 3.7 copy-start.19
  177.7 3.0 copy-start.29
  180.6 55.4 %all-gather.7.cloned.1.call-start = ((), (), s32[]{:S(2)}) async-start(), calls=%async_computation.17 | async-start | bytes 3538944 | tf_op jit(solution)/shard_map/all_gather | solution.py:65
  187.7 92.1 %all-reduce.7.cloned.1.call-start = ((), (), s32[]{:S(2)}) async-start(), calls=%async_computation.10 | async-start | bytes 4718592 | tf_op jit(solution)/shard_map/psum | solution.py:130
  207.0 2.2 copy-start.4
  207.0 2.8 copy-start.35
  207.0 2.7 copy-start.47
  207.0 2.7 copy-start.48
  207.1 84.2 %copy-start.21 = (f32[1536]{0:T(1024)}, f32[1536]{0:T(1024)S(1)}, u32[]{:S(2)}) copy-start(f32[1536]{0:T(1024)S(1)} %broadcast_multiply_fusion) | copy-start | bytes 18436
  249.4 2.1 copy-start.51
  256.6 283.4 %all-reduce.9.cloned.1.call-start = ((), (), s32[]{:S(2)}) async-start(), calls=%async_computation.11 | async-start | bytes 4718592 | tf_op jit(solution)/shard_map/psum | solution.py:191
  279.7 6.2 copy-start.10
  285.1 6.2 copy-start.15
  285.1 6.2 copy-start.26
  285.1 6.2 copy-start.36
  291.3 7.1 copy-start.20
  296.3 2.1 copy-start.9
  310.2 6.5 copy-start.2
  351.8 3.8 copy-start.5
  368.0 6.5 copy-start.2
  410.0 3.7 copy-start.5
  426.2 6.5 copy-start.2
  468.2 3.7 copy-start.5
  476.5 3.4 copy-start.16
  495.8 70.1 %reduce-scatter.16.cloned.1.call-start = ((), (), s32[]{:S(2)}) async-start(), calls=%async_computation.18 | async-start | bytes 3538944
  502.8 2.6 copy-start.14
  505.3 5.5 copy-start.22
  505.3 5.5 copy-start.27
  505.3 5.5 copy-start.37
  505.3 5.5 copy-start.49
  505.4 247.7 %reduce-scatter.10.cloned.1.call-start = ((), (), s32[]{:S(2)}) async-start(), calls=%async_computation.13 | async-start | bytes 1253376 | tf_op jit(solution)/shard_map/reduce_scatter | solution.py:203
  510.5 327.7 %reduce-scatter.12.cloned.1.call-start = ((), (), s32[]{:S(2)}) async-start(), calls=%async_computation.14 | async-start | bytes 5013504 | tf_op jit(solution)/shard_map/reduce_scatter | solution.py:204
  521.2 2.0 copy-start.18
  521.2 2.0 copy-start.24
  521.2 2.0 copy-start.34
  521.2 456.4 %reduce-scatter.8.cloned.1.call-start = ((), (), s32[]{:S(2)}) async-start(), calls=%async_computation.12 | async-start | bytes 3760128 | tf_op jit(solution)/shard_map/reduce_scatter | solution.py:202
  530.2 590.4 %reduce-scatter.14.cloned.1.call-start = ((), (), s32[]{:S(2)}) async-start(), calls=%async_computation.15 | async-start | bytes 5013504 | tf_op jit(solution)/shard_map/reduce_scatter | solution.py:205
  540.0 5.0 copy-start.31
  540.6 4.3 copy-start.12
  548.6 17.3 %copy-start.45 = (f32[768]{0:T(1024)S(1)}, f32[768]{0:T(1024)}, u32[]{:S(2)}) copy-start(f32[768]{0:T(1024)} %param.33) | copy-start | bytes 9220
  558.7 57.6 %all-to-all-start.3 = ((bf16[16,192,384]{2,1,0:T(8,128)(2,1)}), bf16[16,192,384]{2,1,0:T(8,128)(2,1)S(1)}, u32[]{:S(2)}, u32[]{:S(2)}) async-start(bf16[16,192,384]{2,1,0:T(8,128)(2,1)} %bitcast.113), calls=%async_computation.3 | async-start | bytes 4718592 | tf_op jit(solution)/shard_map/all_to_all | solution.py:198
  568.3 59.9 %copy-start.39 = (s32[1536]{0:T(1024)S(1)}, s32[1536]{0:T(1024)}, u32[]{:S(2)}) copy-start(s32[1536]{0:T(1024)} %copy-done.38) | copy-start | bytes 18436
  568.3 59.9 %copy-start.11 = (bf16[3,512,6,64]{1,3,2,0:T(8,128)(2,1)S(1)}, bf16[3,512,6,64]{1,3,2,0:T(8,128)(2,1)}, u32[]{:S(2)}) copy-start(bf16[3,512,6,64]{1,3,2,0:T(8,128)(2,1)} %get-tuple-element.118) | copy-start | bytes 3538948
  616.3 129.7 %all-to-all-start.1 = ((bf16[16,192,384]{2,1,0:T(8,128)(2,1)}), bf16[16,192,384]{2,1,0:T(8,128)(2,1)}, u32[]{:S(2)}, u32[]{:S(2)}) async-start(bf16[16,192,384]{2,1,0:T(8,128)(2,1)} %bitcast.116), calls=%async_computation.1 | async-start | bytes 4718592 | tf_op jit(solution)/shard_map/all_to_all | solution.py:112
  745.9 374.7 %copy-start.1 = (bf16[768,1536]{1,0:T(8,128)(2,1)S(1)}, bf16[768,1536]{1,0:T(8,128)(2,1)}, u32[]{:S(2)}) copy-start(bf16[768,1536]{1,0:T(8,128)(2,1)} %param.30) | copy-start | bytes 7077892
  (10 other events, 10.1 us)
Sparse Core Ops, SparseCore 0:
  80.6 16.3 all-gather.4
  180.7 23.0 all-reduce.4
  205.9 12.0 all-gather.6
  256.7 22.9 all-reduce.6
  495.9 22.9 all-reduce.8
  521.0 11.2 reduce-scatter.15
  537.6 157.0 reduce-scatter.9
  700.5 137.6 reduce-scatter.11
  843.9 133.6 reduce-scatter.7
  983.1 137.4 reduce-scatter.13
where the time goes:
time: 1140 us; the launch traced here: 1130 us
  waiting for transfers between devices  493 us (43%)
  matrix products  233 us (20%)
  other arithmetic  117 us (10%)
  blocking collectives  111 us (10%)
  local copies, waits for them, and re-layouts  107 us (9%)
  starting transfers between devices  40.1 us (4%)
  between operations  15.2 us (1%)
    reduce_scatter x1, waiting for transfers between devices, local(): lax.psum_scatter(down_weight_grad, 'dp', scatter_dimension=1, tiled=True)  143 us
    reduce_scatter x1, waiting for transfers between devices, local(): lax.psum_scatter(qkv_weight_grad, 'dp', scatter_dimension=0, tiled=True)  139 us
    psum x1, blocking collectives, local(): lax.psum((norm1_gain_grad, norm1_bias_grad, qv_bias_grad, out_bias_grad,...  111 us
    reduce_scatter x1, waiting for transfers between devices, local(): lax.psum_scatter(up_weight_grad, 'dp', scatter_dimension=0, tiled=True)  85.1 us
    all_to_all x1, waiting for transfers between devices, local(): lax.all_to_all(send_rows, 'dp', split_axis=0, concat_axis=0, tiled=True)  47.5 us
    dot_general x3, matrix products, attend_back(): jnp.einsum('qhd,khd->hqk', grad_block, value_rows, preferred_element_type...  42.4 us
    convert_element_type x3, other arithmetic, attend_back(): score_grad = (probs * (prob_grad - inner_sum)).astype(jnp.bfloat16)  39.7 us
    all_to_all x1, waiting for transfers between devices, local(): lax.all_to_all(input_slots, 'dp', split_axis=0, concat_axis=0, tiled=True)  38.5 us
  transfers between devices with their start and end apart: 14, of which 7 were waited for; matrix products, arithmetic and copies ran while one was open for 18% of the time, Pallas kernels for 0%

commit v1 on v0

v1 whole, which is shorter than its diff:
```python
import jax
import jax.numpy as jnp
from jax import lax
from jax.sharding import PartitionSpec as P

HEAD_DIM = 64
NORM_EPS = 1e-06
MASK_FILL = -1e30
BF = jnp.bfloat16
F32 = jnp.float32


def dot(a, b, dims):
    return lax.dot_general(a, b, (dims, ((), ())), preferred_element_type=F32)


def norm_stats(values):
    center = values - jnp.mean(values, axis=-1, keepdims=True)
    spread = jnp.mean(center * center, axis=-1, keepdims=True)
    scale = lax.rsqrt(spread + NORM_EPS)
    return center * scale, scale


def norm_back(grad, gain, unit, scale):
    n = grad * gain
    mean_n = jnp.mean(n, axis=-1, keepdims=True)
    mean_nx = jnp.mean(n * unit, axis=-1, keepdims=True)
    return scale * (n - mean_n - unit * mean_nx)


def gelu_pair(u):
    cdf = 0.5 * (1.0 + lax.erf(u * (0.5**0.5)))
    return u * cdf, cdf + u * jnp.exp(-0.5 * u * u) * 0.3989422804014327


def halves(array, index, axis):
    size = array.shape[axis] // 2
    mine = lax.dynamic_slice_in_dim(array, index * size, size, axis)
    other = lax.dynamic_slice_in_dim(array, (1 - index) * size, size, axis)
    return mine, other


def join(mine, other, index, axis):
    first = index == 0
    return jnp.concatenate(
        [jnp.where(first, mine, other), jnp.where(first, other, mine)], axis=axis
    )


def exchange(array, axis_name, bit, size):
    return lax.ppermute(array, axis_name, [(i, i ^ bit) for i in range(size)])


def swap(array):
    return exchange(array, "mp", 1, 2)


def reduce_rows(array, order, dp_index, dp_size):
    rows, columns = array.shape
    bits = dp_size.bit_length() - 1
    view = array.reshape((2,) * bits + (rows // dp_size, columns))
    left = list(range(bits - 1, -1, -1))
    for place, bit in enumerate(order):
        axis = left.index(bit)
        mine = (dp_index >> bit) & 1
        keep = lax.dynamic_index_in_dim(view, mine, axis, keepdims=False)
        send = lax.dynamic_index_in_dim(view, 1 - mine, axis, keepdims=False)
        got = exchange(send, "dp", 1 << bit, dp_size)
        view = keep.astype(F32) + got.astype(F32)
        if place < bits - 1:
            view = view.astype(BF)
        left.remove(bit)
    return view


def masked_scores(query_block, key_rows, clip_block, clip_all, score_scale):
    raw_scores = (
        jnp.einsum("qhd,khd->hqk", query_block, key_rows, preferred_element_type=F32) * score_scale
    )
    same_clip = clip_block[:, None] == clip_all[None, :]
    return jnp.where(same_clip[None], raw_scores, MASK_FILL)


def attend_forward(query, key, value, clip_ids):
    row_count, half_width = query.shape
    heads = half_width // HEAD_DIM
    query_rows, key_rows, value_rows = (
        a.reshape(row_count, heads, HEAD_DIM) for a in (query, key, value)
    )
    score_scale = HEAD_DIM ** (-0.5)
    block_rows = min(512, row_count)

    def attend(block_index):
        start = block_index * block_rows
        query_block = lax.dynamic_slice_in_dim(query_rows, start, block_rows, 0)
        clip_block = lax.dynamic_slice_in_dim(clip_ids, start, block_rows, 0)
        scores = masked_scores(query_block, key_rows, clip_block, clip_ids, score_scale)
        row_max = jnp.max(scores, axis=-1, keepdims=True)
        exponent = jnp.exp(scores - row_max)
        row_total = jnp.sum(exponent, axis=-1, keepdims=True)
        probs_low = (exponent / row_total).astype(BF)
        mixed = jnp.einsum("hqk,khd->qhd", probs_low, value_rows, preferred_element_type=F32)
        return mixed.astype(BF), (row_max + jnp.log(row_total))[..., 0]

    mixed, log_totals = lax.map(attend, jnp.arange(row_count // block_rows))
    return mixed.reshape(row_count, half_width), log_totals


def attend_backward(query, key, value, clip_ids, log_totals, mixed, mixed_grad):
    row_count, half_width = query.shape
    heads = half_width // HEAD_DIM
    query_rows, key_rows, value_rows, mixed_grad = (
        a.reshape(row_count, heads, HEAD_DIM) for a in (query, key, value, mixed_grad)
    )
    score_scale = HEAD_DIM ** (-0.5)
    block_rows = min(512, row_count)

    def back(carried, block_index):
        key_acc, value_acc = carried
        start = block_index * block_rows
        query_block = lax.dynamic_slice_in_dim(query_rows, start, block_rows, 0)
        clip_block = lax.dynamic_slice_in_dim(clip_ids, start, block_rows, 0)
        grad_block = lax.dynamic_slice_in_dim(mixed_grad, start, block_rows, 0)
        scores = masked_scores(query_block, key_rows, clip_block, clip_ids, score_scale)
        probs = jnp.exp(scores - log_totals[block_index][..., None])
        probs_low = probs.astype(BF)
        prob_grad = jnp.einsum("qhd,khd->hqk", grad_block, value_rows, preferred_element_type=F32)
        inner_sum = jnp.sum(prob_grad * probs, axis=-1, keepdims=True)
        score_grad = (probs * (prob_grad - inner_sum)).astype(BF)
        query_grad = (
            jnp.einsum("hqk,khd->qhd", score_grad, key_rows, preferred_element_type=F32)
            * score_scale
        )
        key_acc = (
            key_acc
            + jnp.einsum("hqk,qhd->khd", score_grad, query_block, preferred_element_type=F32)
            * score_scale
        )
        value_acc = value_acc + jnp.einsum(
            "hqk,qhd->khd", probs_low, grad_block, preferred_element_type=F32
        )
        return (key_acc, value_acc), query_grad.astype(BF)

    zero = jnp.zeros((row_count, heads, HEAD_DIM), F32)
    (key_total, value_total), query_blocks = lax.scan(
        back, (zero, zero), jnp.arange(row_count // block_rows)
    )
    parts = (query_blocks, key_total.astype(BF), value_total.astype(BF))
    return jnp.concatenate([p.reshape(row_count, half_width) for p in parts], axis=1)


def to_groups(rows, send_slot, dp_size):
    slots = jnp.zeros((2 * rows.shape[0], rows.shape[1]), BF).at[send_slot].set(rows)
    return lax.all_to_all(slots, "dp", split_axis=0, concat_axis=0, tiled=True)


def to_entry(rows, pack_index, send_slot):
    slots = jnp.zeros((2 * rows.shape[0], rows.shape[1]), BF).at[pack_index].set(rows)
    back = lax.all_to_all(slots, "dp", split_axis=0, concat_axis=0, tiled=True)
    return back[send_slot]


def local(dp_size, *args):
    (
        tokens,
        norm1_gain,
        norm1_bias,
        qkv_weight,
        qv_bias,
        out_weight,
        out_bias,
        norm2_gain,
        norm2_bias,
        up_weight,
        up_bias,
        down_weight,
        down_bias,
        out_grad,
        send_slot,
        pack_index,
        clip_ids,
    ) = args
    row_count, half = tokens.shape
    width = 2 * half
    m = lax.axis_index("mp")
    dp_index = lax.axis_index("dp")
    bits = dp_size.bit_length() - 1
    low_first = list(range(bits))
    swap_first = [1, 0] + low_first[2:]

    out_w_o, up_w_o, down_w_o = swap(out_weight), swap(up_weight), swap(down_weight)
    up_b_o = swap(up_bias)
    qkv_flat = qkv_weight.reshape(width, 3 * half)
    zero_half = jnp.zeros((half,), F32)
    proj_bias = jnp.concatenate([qv_bias[0], zero_half, qv_bias[1]])

    recv_rows = to_groups(tokens, send_slot, dp_size)
    recv_rows, grads_in = lax.optimization_barrier((recv_rows, out_grad))
    recv_grads = to_groups(grads_in, send_slot, dp_size)

    my_index, other_index = halves(pack_index, m, 0)
    turned_index = jnp.concatenate([my_index, other_index])

    x_half = recv_rows[pack_index]
    x_low = join(x_half, swap(x_half), m, 1)
    x = x_low.astype(F32)
    unit1, _ = norm_stats(x)
    h1 = (unit1 * norm1_gain + norm1_bias).astype(BF)
    proj = (dot(h1, qkv_flat, ((1,), (0,))) + proj_bias).astype(BF)
    query, key, value = proj[:, :half], proj[:, half : 2 * half], proj[:, 2 * half :]
    mixed, log_totals = attend_forward(query, key, value, clip_ids)

    mixed_my, mixed_send = halves(mixed, m, 0)
    mixed_o = swap(mixed_send)
    x_my = halves(x_low, m, 0)[0].astype(F32)
    x2 = (
        x_my
        + (dot(mixed_my, out_weight, ((1,), (0,))) + dot(mixed_o, out_w_o, ((1,), (0,))))
        + out_bias
    )
    unit2, scale2 = norm_stats(x2)
    h2 = (unit2 * norm2_gain + norm2_bias).astype(BF)
    g_m, gp_m = gelu_pair(dot(h2, up_weight, ((1,), (0,))) + up_bias)
    g_o, gp_o = gelu_pair(dot(h2, up_w_o, ((1,), (0,))) + up_b_o)
    g_m, g_o, gp_m, gp_o = (a.astype(BF) for a in (g_m, g_o, gp_m, gp_o))
    y = (
        x2 + (dot(g_m, down_weight, ((1,), (0,))) + dot(g_o, down_w_o, ((1,), (0,)))) + down_bias
    ).astype(BF)

    grad_half = recv_grads[turned_index]
    half_rows = row_count // 2
    dy_low = join(grad_half[:half_rows], swap(grad_half[half_rows:]), m, 1)
    dy = dy_low.astype(F32)
    du_m = (dot(dy_low, down_weight, ((1,), (1,))) * gp_m.astype(F32)).astype(BF)
    du_o = (dot(dy_low, down_w_o, ((1,), (1,))) * gp_o.astype(F32)).astype(BF)
    dh2 = dot(du_m, up_weight, ((1,), (1,))) + dot(du_o, up_w_o, ((1,), (1,)))
    dx2 = dy + norm_back(dh2, norm2_gain, unit2, scale2)
    da = dx2.astype(BF)
    do_m = dot(da, out_weight, ((1,), (1,))).astype(BF)
    do_o = dot(da, out_w_o, ((1,), (1,))).astype(BF)
    do = join(do_m, swap(do_o), m, 0)

    y_my, y_send = halves(y, m, 1)
    out = to_entry(jnp.concatenate([y_my, swap(y_send)]), turned_index, send_slot)

    first = lambda a, b: dot(a, b, ((0,), (0,)))
    up_grad_o = swap(first(h2, du_o).astype(BF))
    down_grad_o = swap(first(dy_low, g_o).astype(BF))
    out_grad_o = swap(first(da, mixed_o).astype(BF))
    up_grad = (first(h2, du_m) + up_grad_o.astype(F32)).astype(BF)
    down_grad = (first(dy_low, g_m) + down_grad_o.astype(F32)).astype(BF)
    out_w_grad = (first(da, mixed_my) + out_grad_o.astype(F32)).astype(BF)
    up_grad = reduce_rows(up_grad, low_first, dp_index, dp_size)
    down_grad = reduce_rows(down_grad, swap_first, dp_index, dp_size)
    out_w_grad = reduce_rows(out_w_grad, swap_first, dp_index, dp_size)

    d_proj = attend_backward(query, key, value, clip_ids, log_totals, mixed, do)

    dp_my, dp_send = halves(d_proj, m, 0)
    dh1_send = dot(dp_send, qkv_flat, ((1,), (1,))).astype(BF)
    dh1 = dot(dp_my, qkv_flat, ((1,), (1,))) + swap(dh1_send).astype(F32)
    unit1_my, scale1_my = norm_stats(x_my)
    dx = (dx2 + norm_back(dh1, norm1_gain, unit1_my, scale1_my)).astype(BF)
    dx_my, dx_send = halves(dx, m, 1)
    tokens_grad = to_entry(jnp.concatenate([dx_my, swap(dx_send)]), turned_index, send_slot)

    qkv_grad = first(h1, d_proj).astype(BF)
    qkv_grad = reduce_rows(qkv_grad, low_first, dp_index, dp_size)

    total = lambda a: jnp.sum(a.astype(F32), axis=0)
    shared = [
        total(dh1 * unit1_my),
        total(dh1),
        total(dx2),
        total(dh2 * unit2),
        total(dh2),
        total(dy),
    ]
    both = jnp.concatenate(shared + [total(du_m)])
    both = both + swap(jnp.concatenate(shared + [total(du_o)]))
    small = jnp.concatenate([both, total(d_proj)])
    for bit in range(bits):
        small = small + exchange(small, "dp", 1 << bit, dp_size)
    n1g, n1b, ob, n2g, n2b, db = (small[i * width : (i + 1) * width] for i in range(6))
    rest = small[6 * width :]
    hidden = up_bias.shape[0]
    up_b_grad, proj_b_grad = rest[:hidden], rest[hidden:]
    qv_grad = jnp.stack([proj_b_grad[:half], proj_b_grad[2 * half :]])

    return (
        out,
        tokens_grad,
        n1g,
        n1b,
        qkv_grad.reshape(-1, 3, half),
        qv_grad,
        out_w_grad.T,
        ob,
        n2g,
        n2b,
        up_grad,
        up_b_grad,
        down_grad.T,
        db,
    )


def solution(mesh):
    dp_size = mesh.shape["dp"]
    in_specs = (
        P("dp", "mp"),
        P(),
        P(),
        P(None, None, "mp"),
        P(None, "mp"),
        P("mp", None),
        P(),
        P(),
        P(),
        P(None, "mp"),
        P("mp"),
        P("mp", None),
        P(),
        P("dp", "mp"),
        P("dp"),
        P("dp"),
        P("dp"),
    )
    out_specs = (
        P("dp", "mp"),
        P("dp", "mp"),
        P(),
        P(),
        P("dp", None, "mp"),
        P(None, "mp"),
        P("mp", "dp"),
        P(),
        P(),
        P(),
        P("dp", "mp"),
        P("mp"),
        P("mp", "dp"),
        P(),
    )

    def run(*args):
        return local(dp_size, *args)

    return jax.shard_map(run, mesh=mesh, in_specs=in_specs, out_specs=out_specs, check_vma=False)
```

time: 1140 us -> 654 us (0.57)
  waiting for transfers between devices: 493 us -> 155 us
  blocking collectives: 111 us -> 0 us
  starting transfers between devices: 40.1 us -> 70.7 us
  matrix products: 233 us -> 205 us
  other arithmetic: 117 us -> 104 us
  between operations: 15.2 us -> 2.24 us
    reduce_scatter x4 -> x0, waiting for transfers between devices: 368 us -> none  [the longest x1 143 us: local(): lax.psum_scatter(down_weight_grad, 'dp', scatter_dimension=1, tiled=True)]
    psum x1 -> x0, blocking collectives: 111 us -> none  [local(): lax.psum((norm1_gain_grad, norm1_bias_grad, qv_bias_grad, out_bias_grad,...]
    ppermute x0 -> x35, waiting for transfers between devices: none -> 86.2 us  [exchange(): return lax.ppermute(array, axis_name, [(i, i ^ bit) for i in range(size)])]
    psum x3 -> x0, waiting for transfers between devices: 39.1 us -> none  [the longest x1 23 us: local(): lax.psum(normed_two_terms.astype(jnp.bfloat16), 'mp').astype(jnp.float32)]
    ppermute x0 -> x35, starting transfers between devices: none -> 35.1 us  [exchange(): return lax.ppermute(array, axis_name, [(i, i ^ bit) for i in range(size)])]
    dot_general x24 -> x34, matrix products: 186 us -> 159 us  [the longest x22 73.1 us: dot(): return lax.dot_general(a, b, (dims, ((), ())), preferred_element_type=F32)]
    reduce_sum x11 -> x7, other arithmetic: 33.2 us -> 8.08 us  [the longest x3 3.03 us: norm_stats(): spread = jnp.mean(center * center, axis=-1, keepdims=True)]
    all_to_all x4, waiting for transfers between devices: 86 us -> 68.8 us  [the longest x2 68.8 us: to_groups(): return lax.all_to_all(slots, 'dp', split_axis=0, concat_axis=0, tiled=True)]
  transfers between devices with their start and end apart: 14 -> 39, of which waited for: 7 -> 17; matrix products, arithmetic and copies ran while one was open for 18% -> 56% of each run, Pallas kernels for 0% -> 0%
where the time goes in v1:
time: 654 us; the launch traced here: 649 us
  matrix products  205 us (31%)
  waiting for transfers between devices  155 us (24%)
  other arithmetic  104 us (16%)
  local copies, waits for them, and re-layouts  102 us (16%)
  starting transfers between devices  70.7 us (11%)
  loops' own time  10.2 us (2%)
    ppermute x35, waiting for transfers between devices, exchange(): return lax.ppermute(array, axis_name, [(i, i ^ bit) for i in range(size)])  86.2 us
    dot_general x22, matrix products, dot(): return lax.dot_general(a, b, (dims, ((), ())), preferred_element_type=F32)  73.1 us
    all_to_all x2, waiting for transfers between devices, to_groups(): return lax.all_to_all(slots, 'dp', split_axis=0, concat_axis=0, tiled=True)  68.8 us
    dot_general x3, matrix products, back(): jnp.einsum('qhd,khd->hqk', grad_block, value_rows, preferred_element_type...  42.5 us
    convert_element_type x3, other arithmetic, back(): score_grad = (probs * (prob_grad - inner_sum)).astype(BF)  39.7 us
    ppermute x35, starting transfers between devices, exchange(): return lax.ppermute(array, axis_name, [(i, i ^ bit) for i in range(size)])  35.1 us
    dot_general x6, matrix products, masked_scores(): jnp.einsum('qhd,khd->hqk', query_block, key_rows, preferred_element_type=...  24.4 us
    dot_general x3, matrix products, back(): jnp.einsum('hqk,qhd->khd', probs_low, grad_block, preferred_element_type=...  23.9 us
  transfers between devices with their start and end apart: 39, of which 17 were waited for; matrix products, arithmetic and copies ran while one was open for 56% of the time, Pallas kernels for 0%

profile of v1, /device:TPU:0, one launch (start us, length us, event | category | flops | bytes accessed | tf_op | source)
XLA Modules:
  0.0 648.9 jit_solution(15415634852332337035)
XLA Ops:
  1.4 9.4 %scatter_custom_fusion = bf16[3072,384]{1,0:T(8,128)(2,1)} fusion(s32[1536]{0:T(1024)S(1)} %get-tuple-element.301, bf16[1536,384]{1,0:T(8,128)(2,1)} %param.21, bf16[]{:T(256)} %constant.178.clone.1), kind=kCustom, calls=%fused_computation.159 | custom fusion | bytes 2359808 | tf_op jit(solution)/shard_map/scatter | solution.py:153
  10.7 8.5 %all-to-all-start = ((bf16[16,192,384]{2,1,0:T(8,128)(2,1)}), bf16[16,192,384]{2,1,0:T(8,128)(2,1)S(1)}, u32[]{:S(2)}, u32[]{:S(2)}) async-start(bf16[16,192,384]{2,1,0:T(8,128)(2,1)} %bitcast.238), calls=%async_computation | async-start | bytes 4718592 | tf_op jit(solution)/shard_map/all_to_all | solution.py:154
  19.3 47.5 %all-to-all-done = bf16[16,192,384]{2,1,0:T(8,128)(2,1)S(1)} async-done(((bf16[16,192,384]{2,1,0:T(8,128)(2,1)}), bf16[16,192,384]{2,1,0:T(8,128)(2,1)S(1)}, u32[]{:S(2)}, u32[]{:S(2)}) %all-to-all-start) | async-done | bytes 2359328 | tf_op jit(solution)/shard_map/all_to_all | solution.py:154
  66.8 4.7 gather_fusion
  79.2 3.6 fusion.38
  85.2 56.7 %while.27 = (s32[]{:T(128)}, bf16[3,512,6,64]{1,3,2,0:T(8,128)(2,1)}, f32[3,6,512]{2,1,0:T(8,128)}, s32[3]{0:T(128)S(1)}, s32[1536]{0:T(1024)S(1)}, /*index=5*/b...) while((s32[]{:T(128)}, ...), condition=%wide.region_6.7_spmd, body=%wide.region_3.6_spmd.sunk | while | flops 1265562624 | bytes 63029448 | solution.py:105
  87.0 4.5 fusion.190
  91.5 4.9 fusion.191
  96.4 7.1 %fusion.192 = bf16[3,512,6,64]{1,3,2,0:T(8,128)(2,1)} fusion(bf16[3,512,6,64]{1,3,2,0:T(8,128)(2,1)} %get-tuple-element.439, s32[]{:T(128)S(6)} %copy.87, bf16[1536,6,64]{0,2,1:T(8,128)(2,1)S(1)} %get-tuple-element.457, f32[6,512,1536]{2,1,0:T(8,128)S(1)} %get-tuple-element.411, f32[6,512]{1,0:T(8,128)S(1)} %fusion.191, ...), kind=kOutput, calls=%fused_computation.17.clone.1 | convolution fusion | flops 627769344 | bytes 21258244 | tf_op jit(solution)/shard_map/while/body/eval_jaxpr/hqk,khd->qhd/dot_general | solution.py:102
  105.9 4.5 fusion.190
  110.4 4.9 fusion.191
  115.3 7.1 %fusion.192 = bf16[3,512,6,64]{1,3,2,0:T(8,128)(2,1)} fusion(bf16[3,512,6,64]{1,3,2,0:T(8,128)(2,1)} %get-tuple-element.439, s32[]{:T(128)S(6)} %copy.87, bf16[1536,6,64]{0,2,1:T(8,128)(2,1)S(1)} %get-tuple-element.457, f32[6,512,1536]{2,1,0:T(8,128)S(1)} %get-tuple-element.411, f32[6,512]{1,0:T(8,128)S(1)} %fusion.191, ...), kind=kOutput, calls=%fused_computation.17.clone.1 | convolution fusion | flops 627769344 | bytes 21258244 | tf_op jit(solution)/shard_map/while/body/eval_jaxpr/hqk,khd->qhd/dot_general | solution.py:102
  124.8 4.5 fusion.190
  129.3 4.9 fusion.191
  134.2 7.1 %fusion.192 = bf16[3,512,6,64]{1,3,2,0:T(8,128)(2,1)} fusion(bf16[3,512,6,64]{1,3,2,0:T(8,128)(2,1)} %get-tuple-element.439, s32[]{:T(128)S(6)} %copy.87, bf16[1536,6,64]{0,2,1:T(8,128)(2,1)S(1)} %get-tuple-element.457, f32[6,512,1536]{2,1,0:T(8,128)S(1)} %get-tuple-element.411, f32[6,512]{1,0:T(8,128)S(1)} %fusion.191, ...), kind=kOutput, calls=%fused_computation.17.clone.1 | convolution fusion | flops 627769344 | bytes 21258244 | tf_op jit(solution)/shard_map/while/body/eval_jaxpr/hqk,khd->qhd/dot_general | solution.py:102
  148.5 9.8 %scatter_custom_fusion.2 = bf16[3072,384]{1,0:T(8,128)(2,1)} fusion(s32[1536]{0:T(1024)} %copy-done.39, bf16[1536,384]{1,0:T(8,128)(2,1)} %param.34, bf16[]{:T(256)} %constant.178.clone.1), kind=kCustom, calls=%fused_computation.156 | custom fusion | bytes 2359808 | tf_op jit(solution)/shard_map/scatter | solution.py:153
  158.3 11.1 %all-to-all-start.2 = ((bf16[16,192,384]{2,1,0:T(8,128)(2,1)}), bf16[16,192,384]{2,1,0:T(8,128)(2,1)}, u32[]{:S(2)}, u32[]{:S(2)}) async-start(bf16[16,192,384]{2,1,0:T(8,128)(2,1)} %bitcast.237), calls=%async_computation.2 | async-start | bytes 4718592 | tf_op jit(solution)/shard_map/all_to_all | solution.py:154
  177.4 5.0 multiply_convert_fusion.4
  184.4 5.6 multiply_convert_fusion.3
  190.1 4.5 add_convert_fusion.2
  195.8 21.3 %all-to-all-done.2 = bf16[16,192,384]{2,1,0:T(8,128)(2,1)} async-done(((bf16[16,192,384]{2,1,0:T(8,128)(2,1)}), bf16[16,192,384]{2,1,0:T(8,128)(2,1)}, u32[]{:S(2)}, u32[]{:S(2)}) %all-to-all-start.2) | async-done | bytes 2359328 | tf_op jit(solution)/shard_map/all_to_all | solution.py:154
  217.1 7.2 %gather_fusion.2 = bf16[1536,384]{1,0:T(8,128)(2,1)} fusion(bf16[3072,384]{1,0:T(8,128)(2,1)} %bitcast.13, s32[2048]{0:T(1024)} %pad_clamp_fusion), kind=kCustom, calls=%fused_computation.2 | custom fusion | bytes 2365440 | tf_op jit(solution)/shard_map/gather | solution.py:230
  230.0 9.8 %scatter_custom_fusion.1 = bf16[3072,384]{1,0:T(8,128)(2,1)} fusion(s32[1536]{0:T(1024)} %fusion.116, bf16[768,384]{1,0:T(8,128)(2,1)} %collective-permute-done.6, bf16[]{:T(256)} %constant.209, bf16[768,384]{1,0:T(8,128)(2,1)} %get-tuple-element.262, bf16[]{:T(256)} %constant.178.clone.1), kind=kCustom, calls=%fused_computation.136 | custom fusion | flops 2359296 | bytes 3539968 | tf_op jit(solution)/shard_map/scatter | solution.py:158
  239.8 11.5 %all-to-all-start.1 = ((bf16[16,192,384]{2,1,0:T(8,128)(2,1)}), bf16[16,192,384]{2,1,0:T(8,128)(2,1)}, u32[]{:S(2)}, u32[]{:S(2)}) async-start(bf16[16,192,384]{2,1,0:T(8,128)(2,1)} %bitcast.235), calls=%async_computation.1 | async-start | bytes 4718592 | tf_op jit(solution)/shard_map/all_to_all | solution.py:159
  253.4 6.8 %convert_reduce_fusion.3 = (f32[1536]{0:T(1024)}, bf16[768,1536]{1,0:T(8,128)(2,1)S(1)}) fusion(f32[768,1536]{1,0:T(8,128)} %get-tuple-element.291, f32[1536]{0:T(1024)} %param.31, bf16[1536,768]{1,0:T(8,128)(2,1)S(1)} %copy-done.59, bf16[768,384]{1,0:T(8,128)(2,1)S(1)} %get-tuple-element.256, bf16[768,384]{1,0:T(8,128)(2,1)S(1)} %get-tuple-element.255), kind=kOutput, calls=%fused_computation.79 | convolution fusion | flops 1831991808 | bytes 10629120 | tf_op jit(solution)/shard_map/dot_general | solution.py:14
  262.3 5.4 convert_reduce_fusion.2
  267.7 4.9 multiply_reduce_fusion.1
  282.0 3.4 convolution_convert_fusion.1
  290.3 170.1 %while.28 = (s32[]{:T(128)}, f32[1536,6,64]{0,2,1:T(8,128)S(1)}, f32[1536,6,64]{0,2,1:T(8,128)}, bf16[3,512,6,64]{1,3,2,0:T(8,128)(2,1)}, s32[3]{0:T(128)S(1)}, ...) while((s32[]{:T(128)}, f32[1536,6,64]{0,2,1:T(8,128)S(1)}, ...), condition=%wide.region_17.18_spmd.clone, body=%wide.region_15.17_spmd.clone.sunk | while | flops 3094803456 | bytes 235241776 | solution.py:145
  295.2 3.6 fusion.202
  298.8 6.4 copy-done
  305.3 7.7 %fusion.204 = f32[1536,6,64]{0,2,1:T(8,128)} fusion(f32[6,512,1536]{2,1,0:T(8,128)S(1)} %fusion.202, f32[6,512]{1,0:T(8,128)S(1)} %dynamic-slice_bitcast_fusion.14, pred[512,1536]{1,0:T(8,128)(4,1)S(1)} %broadcast_compare_fusion.5, f32[1536,6,64]{0,2,1:T(8,128)} %get-tuple-element.480, pred[]{:T(512)S(6)} %compare.3, ...), kind=kOutput, calls=%fused_computation.34.clone.1 | convolution fusion | flops 624033792 | bytes 24784900 | tf_op jit(solution)/shard_map/while/body/eval_jaxpr/hqk,qhd->khd/dot_general | solution.py:139
  312.9 14.2 %multiply_reduce_fusion.7 = (f32[6,512]{1,0:T(8,128)S(1)}, f32[6,512,1536]{2,1,0:T(8,128)}) fusion(f32[6,512,1536]{2,1,0:T(8,128)} %copy-done, f32[6,512]{1,0:T(8,128)S(1)} %dynamic-slice_bitcast_fusion.14, pred[512,1536]{1,0:T(8,128)(4,1)S(1)} %broadcast_compare_fusion.5, bf16[1536,6,64]{0,2,1:T(8,128)(2,1)} %get-tuple-element.504, ...), kind=kOutput, calls=%fused_computation.25.clone.1 | convolution fusion | flops 627569664 | bytes 40132612 | tf_op jit(solution)/shard_map/while/body/eval_jaxpr/qhd,khd->hqk/dot_general | solution.py:127
  327.1 13.2 %multiply_convert_fusion.6 = bf16[6,512,1536]{2,1,0:T(8,128)(2,1)S(1)} fusion(f32[6,512,1536]{2,1,0:T(8,128)} %get-tuple-element.424, f32[6,512,1536]{2,1,0:T(8,128)} %copy-done, f32[6,512]{1,0:T(8,128)S(1)} %get-tuple-element.425, f32[6,512]{1,0:T(8,128)S(1)} %dynamic-slice_bitcast_fusion.14, pred[512,1536]{1,0:T(8,128)(4,1)S(1)} %broadcast_compare_fusion.5), kind=kLoop, calls=%fused_computation.24.clone.1 | loop fusion | flops 28311552 | bytes 47996928 | tf_op jit(solution)/shard_map/while/body/eval_jaxpr/convert_element_type | solution.py:129
  340.3 3.7 fusion.205
  351.4 3.6 fusion.202
  355.0 6.4 copy-done
  361.5 8.1 %fusion.204 = f32[1536,6,64]{0,2,1:T(8,128)} fusion(f32[6,512,1536]{2,1,0:T(8,128)S(1)} %fusion.202, f32[6,512]{1,0:T(8,128)S(1)} %dynamic-slice_bitcast_fusion.14, pred[512,1536]{1,0:T(8,128)(4,1)S(1)} %broadcast_compare_fusion.5, f32[1536,6,64]{0,2,1:T(8,128)} %get-tuple-element.480, pred[]{:T(512)S(6)} %compare.3, ...), kind=kOutput, calls=%fused_computation.34.clone.1 | convolution fusion | flops 624033792 | bytes 24784900 | tf_op jit(solution)/shard_map/while/body/eval_jaxpr/hqk,qhd->khd/dot_general | solution.py:139
  369.6 14.1 %multiply_reduce_fusion.7 = (f32[6,512]{1,0:T(8,128)S(1)}, f32[6,512,1536]{2,1,0:T(8,128)}) fusion(f32[6,512,1536]{2,1,0:T(8,128)} %copy-done, f32[6,512]{1,0:T(8,128)S(1)} %dynamic-slice_bitcast_fusion.14, pred[512,1536]{1,0:T(8,128)(4,1)S(1)} %broadcast_compare_fusion.5, bf16[1536,6,64]{0,2,1:T(8,128)(2,1)} %get-tuple-element.504, ...), kind=kOutput, calls=%fused_computation.25.clone.1 | convolution fusion | flops 627569664 | bytes 40132612 | tf_op jit(solution)/shard_map/while/body/eval_jaxpr/qhd,khd->hqk/dot_general | solution.py:127
  383.7 13.2 %multiply_convert_fusion.6 = bf16[6,512,1536]{2,1,0:T(8,128)(2,1)S(1)} fusion(f32[6,512,1536]{2,1,0:T(8,128)} %get-tuple-element.424, f32[6,512,1536]{2,1,0:T(8,128)} %copy-done, f32[6,512]{1,0:T(8,128)S(1)} %get-tuple-element.425, f32[6,512]{1,0:T(8,128)S(1)} %dynamic-slice_bitcast_fusion.14, pred[512,1536]{1,0:T(8,128)(4,1)S(1)} %broadcast_compare_fusion.5), kind=kLoop, calls=%fused_computation.24.clone.1 | loop fusion | flops 28311552 | bytes 47996928 | tf_op jit(solution)/shard_map/while/body/eval_jaxpr/convert_element_type | solution.py:129
  397.0 3.7 fusion.205
  408.0 3.6 fusion.202
  411.7 6.4 copy-done
  418.1 8.1 %fusion.204 = f32[1536,6,64]{0,2,1:T(8,128)} fusion(f32[6,512,1536]{2,1,0:T(8,128)S(1)} %fusion.202, f32[6,512]{1,0:T(8,128)S(1)} %dynamic-slice_bitcast_fusion.14, pred[512,1536]{1,0:T(8,128)(4,1)S(1)} %broadcast_compare_fusion.5, f32[1536,6,64]{0,2,1:T(8,128)} %get-tuple-element.480, pred[]{:T(512)S(6)} %compare.3, ...), kind=kOutput, calls=%fused_computation.34.clone.1 | convolution fusion | flops 624033792 | bytes 24784900 | tf_op jit(solution)/shard_map/while/body/eval_jaxpr/hqk,qhd->khd/dot_general | solution.py:139
  426.2 14.2 %multiply_reduce_fusion.7 = (f32[6,512]{1,0:T(8,128)S(1)}, f32[6,512,1536]{2,1,0:T(8,128)}) fusion(f32[6,512,1536]{2,1,0:T(8,128)} %copy-done, f32[6,512]{1,0:T(8,128)S(1)} %dynamic-slice_bitcast_fusion.14, pred[512,1536]{1,0:T(8,128)(4,1)S(1)} %broadcast_compare_fusion.5, bf16[1536,6,64]{0,2,1:T(8,128)(2,1)} %get-tuple-element.504, ...), kind=kOutput, calls=%fused_computation.25.clone.1 | convolution fusion | flops 627569664 | bytes 40132612 | tf_op jit(solution)/shard_map/while/body/eval_jaxpr/qhd,khd->hqk/dot_general | solution.py:127
  440.4 13.2 %multiply_convert_fusion.6 = bf16[6,512,1536]{2,1,0:T(8,128)(2,1)S(1)} fusion(f32[6,512,1536]{2,1,0:T(8,128)} %get-tuple-element.424, f32[6,512,1536]{2,1,0:T(8,128)} %copy-done, f32[6,512]{1,0:T(8,128)S(1)} %get-tuple-element.425, f32[6,512]{1,0:T(8,128)S(1)} %dynamic-slice_bitcast_fusion.14, pred[512,1536]{1,0:T(8,128)(4,1)S(1)} %broadcast_compare_fusion.5), kind=kLoop, calls=%fused_computation.24.clone.1 | loop fusion | flops 28311552 | bytes 47996928 | tf_op jit(solution)/shard_map/while/body/eval_jaxpr/convert_element_type | solution.py:129
  453.7 3.7 fusion.205
  469.2 4.0 convolution_convert_fusion.2
  487.0 3.5 convolution_convert_fusion
  491.7 9.6 %collective-permute-done.16 = bf16[2,2,2,48,1152]{4,3,0,1,2:T(8,128)(2,1)S(1)} collective-permute-done((bf16[2,2,2,48,1152]{4,3,0,1,2:T(8,128)(2,1)S(1)}, bf16[2,2,2,48,1152]{4,3,0,1,2:T(8,128)(2,1)S(1)}, u32[]{:S(2)}, u32[]{:S(2)}) %collective-permute-start.16) | collective-permute-done | bytes 884768 | tf_op jit(solution)/shard_map/ppermute | solution.py:51
  511.8 3.3 collective-permute-done.13
  522.7 7.0 %gather_fusion.1 = bf16[1536,384]{1,0:T(8,128)(2,1)} fusion(bf16[3072,384]{1,0:T(8,128)(2,1)} %bitcast.11, s32[2048]{0:T(1024)S(1)} %copy-done.32), kind=kCustom, calls=%fused_computation.1 | custom fusion | bytes 2365440 | tf_op jit(solution)/shard_map/gather | solution.py:160
  532.3 6.6 %collective-permute-done.18 = bf16[2,48,1152]{2,1,0:T(8,128)(2,1)S(1)} collective-permute-done((bf16[2,48,1152]{2,1,0:T(8,128)(2,1)S(1)}, bf16[2,48,1152]{2,1,0:T(8,128)(2,1)S(1)}, u32[]{:S(2)}, u32[]{:S(2)}) %collective-permute-start.18) | collective-permute-done | bytes 221216 | tf_op jit(solution)/shard_map/ppermute | solution.py:51
  539.7 3.7 add_convert_fusion
  545.8 3.7 add_convert_fusion.1
  554.0 9.7 %scatter_custom_fusion.3 = bf16[3072,384]{1,0:T(8,128)(2,1)} fusion(s32[1536]{0:T(1024)} %fusion.116, bf16[768,384]{1,0:T(8,128)(2,1)} %collective-permute-done.10, bf16[]{:T(256)} %constant.209, bf16[768,384]{1,0:T(8,128)(2,1)S(1)} %copy-done.21, bf16[]{:T(256)} %constant.178.clone.1), kind=kCustom, calls=%fused_computation.142 | custom fusion | flops 2359296 | bytes 3539968 | tf_op jit(solution)/shard_map/scatter | solution.py:158
  563.7 4.4 all-to-all-start.3
  568.1 9.3 %collective-permute-done.31 = bf16[2,2,2,48,1536]{4,3,0,1,2:T(8,128)(2,1)} collective-permute-done((bf16[2,2,2,48,1536]{4,3,0,1,2:T(8,128)(2,1)}, bf16[2,2,2,48,1536]{4,3,0,1,2:T(8,128)(2,1)}, u32[]{:S(2)}, u32[]{:S(2)}) %collective-permute-start.31) | collective-permute-done | bytes 1179680 | tf_op jit(solution)/shard_map/ppermute | solution.py:51
  583.7 33.5 %collective-permute-done.32 = bf16[2,2,48,1536]{3,2,0,1:T(8,128)(2,1)S(1)} collective-permute-done((bf16[2,2,48,1536]{3,2,0,1:T(8,128)(2,1)S(1)}, bf16[2,2,48,1536]{3,2,0,1:T(8,128)(2,1)S(1)}, u32[]{:S(2)}, u32[]{:S(2)}) %collective-permute-start.32) | collective-permute-done | bytes 589856 | tf_op jit(solution)/shard_map/ppermute | solution.py:51
  619.7 6.8 %collective-permute-done.33 = bf16[2,48,1536]{2,1,0:T(8,128)(2,1)S(1)} collective-permute-done((bf16[2,48,1536]{2,1,0:T(8,128)(2,1)S(1)}, bf16[2,48,1536]{2,1,0:T(8,128)(2,1)S(1)}, u32[]{:S(2)}, u32[]{:S(2)}) %collective-permute-start.33) | collective-permute-done | bytes 294944 | tf_op jit(solution)/shard_map/ppermute | solution.py:51
  626.6 3.3 collective-permute-start.34
  631.3 5.0 collective-permute-start.29
  637.1 5.5 collective-permute-done.29
  643.4 5.3 gather_fusion.3
  (364 shorter events, 135.3 us)
Async XLA Ops:
  1.4 9.4 %copy-start.39 = (s32[1536]{0:T(1024)}, s32[1536]{0:T(1024)S(1)}, u32[]{:S(2)}) copy-start(s32[1536]{0:T(1024)S(1)} %get-tuple-element.301) | copy-start | bytes 18436
  10.7 56.0 %all-to-all-start = ((bf16[16,192,384]{2,1,0:T(8,128)(2,1)}), bf16[16,192,384]{2,1,0:T(8,128)(2,1)S(1)}, u32[]{:S(2)}, u32[]{:S(2)}) async-start(bf16[16,192,384]{2,1,0:T(8,128)(2,1)} %bitcast.238), calls=%async_computation | async-start | bytes 4718592 | tf_op jit(solution)/shard_map/all_to_all | solution.py:154
  71.5 4.8 collective-permute-start
  71.6 112.8 %collective-permute-start.4 = (f32[1536]{0:T(1024)}, f32[1536]{0:T(1024)}, u32[]{:S(2)}, u32[]{:S(2)}) collective-permute-start(f32[1536]{0:T(1024)} %param.31), channel_id=1, source_target_pairs={{0,1},{1,0},{2,3},{3,2},{4,5},{5,4},{6,7},{7,6},{8,9},{9,8},{10,11... | collective-permute-start | bytes 18440 | tf_op jit(solution)/shard_map/ppermute | solution.py:51
  72.1 100.5 %collective-permute-start.2 = (bf16[384,768]{1,0:T(8,128)(2,1)}, bf16[384,768]{1,0:T(8,128)(2,1)}, u32[]{:S(2)}, u32[]{:S(2)}) collective-permute-start(bf16[384,768]{1,0:T(8,128)(2,1)} %param.26), channel_id=1, source_target_pairs={{0,1},{1,0},{2,3},{3,2},{4,5},{5,4},{6,7},{7,6},{8,9},{9,8},{10,11... | collective-permute-start | bytes 1769480 | tf_op jit(solution)/shard_map/ppermute | solution.py:51
  72.1 112.3 %collective-permute-start.3 = (bf16[768,1536]{1,0:T(8,128)(2,1)}, bf16[768,1536]{1,0:T(8,128)(2,1)}, u32[]{:S(2)}, u32[]{:S(2)}) collective-permute-start(bf16[768,1536]{1,0:T(8,128)(2,1)} %param.30), channel_id=1, source_target_pairs={{0,1},{1,0},{2,3},{3,2},{4,5},{5,4},{6,7},{7,6},{8,9},{9,8},{10,11... | collective-permute-start | bytes 7077896 | tf_op jit(solution)/shard_map/ppermute | solution.py:51
  72.6 117.5 %collective-permute-start.5 = (bf16[1536,768]{1,0:T(8,128)(2,1)}, bf16[1536,768]{1,0:T(8,128)(2,1)}, u32[]{:S(2)}, u32[]{:S(2)}) collective-permute-start(bf16[1536,768]{1,0:T(8,128)(2,1)} %param.32), channel_id=1, source_target_pairs={{0,1},{1,0},{2,3},{3,2},{4,5},{5,4},{6,7},{7,6},{8,9},{9,8},{10,11... | collective-permute-start | bytes 7077896 | tf_op jit(solution)/shard_map/ppermute | solution.py:51
  141.9 6.0 copy-start.1
  146.9 25.7 %collective-permute-start.1 = (bf16[768,384]{0,1:T(8,128)(2,1)}, bf16[768,384]{0,1:T(8,128)(2,1)}, u32[]{:S(2)}, u32[]{:S(2)}) collective-permute-start(bf16[768,384]{0,1:T(8,128)(2,1)} %constant_dynamic-slice_fusion.12), channel_id=1, source_target_pairs={{0,1},{1,0},{2,3},{3,2},{4,5},{5,4},{6,7},{7,6},{8,9},{9,8},{10,11... | collective-permute-start | bytes 1769480 | tf_op jit(solution)/shard_map/ppermute | solution.py:51
  158.3 58.8 %all-to-all-start.2 = ((bf16[16,192,384]{2,1,0:T(8,128)(2,1)}), bf16[16,192,384]{2,1,0:T(8,128)(2,1)}, u32[]{:S(2)}, u32[]{:S(2)}) async-start(bf16[16,192,384]{2,1,0:T(8,128)(2,1)} %bitcast.237), calls=%async_computation.2 | async-start | bytes 4718592 | tf_op jit(solution)/shard_map/all_to_all | solution.py:154
  174.9 15.2 %copy-start.2 = (f32[768,768]{1,0:T(8,128)}, f32[768,768]{1,0:T(8,128)S(1)}, u32[]{:S(2)}) copy-start(f32[768,768]{1,0:T(8,128)S(1)} %get-tuple-element.289) | copy-start | bytes 7077892
  177.4 7.0 %copy-start.25 = (bf16[768,768]{1,0:T(8,128)(2,1)}, bf16[768,768]{1,0:T(8,128)(2,1)S(1)}, u32[]{:S(2)}) copy-start(bf16[768,768]{1,0:T(8,128)(2,1)S(1)} %add_convert_fusion.3) | copy-start | bytes 3538948
  184.4 5.7 copy-start.63
  195.8 34.1 %collective-permute-start.6 = (bf16[768,384]{1,0:T(8,128)(2,1)}, bf16[768,384]{1,0:T(8,128)(2,1)}, u32[]{:S(2)}, u32[]{:S(2)}) collective-permute-start(bf16[768,384]{1,0:T(8,128)(2,1)} %get-tuple-element.263), channel_id=1, source_target_pairs={{0,1},{1,0},{2,3},{3,2},{4,5},{5,4},{6,7},{7,6},{8,9},{9,8},{10,11... | collective-permute-start | bytes 1769480 | tf_op jit(solution)/shard_map/ppermute | solution.py:51
  226.3 25.1 %collective-permute-start.7 = (bf16[768,384]{1,0:T(8,128)(2,1)}, bf16[768,384]{1,0:T(8,128)(2,1)}, u32[]{:S(2)}, u32[]{:S(2)}) collective-permute-start(bf16[768,384]{1,0:T(8,128)(2,1)} %slice.82), channel_id=1, source_target_pairs={{0,1},{1,0},{2,3},{3,2},{4,5},{5,4},{6,7},{7,6},{8,9},{9,8},{10,11... | collective-permute-start | bytes 1769480 | tf_op jit(solution)/shard_map/ppermute | solution.py:51
  239.8 282.8 %all-to-all-start.1 = ((bf16[16,192,384]{2,1,0:T(8,128)(2,1)}), bf16[16,192,384]{2,1,0:T(8,128)(2,1)}, u32[]{:S(2)}, u32[]{:S(2)}) async-start(bf16[16,192,384]{2,1,0:T(8,128)(2,1)} %bitcast.235), calls=%async_computation.1 | async-start | bytes 4718592 | tf_op jit(solution)/shard_map/all_to_all | solution.py:159
  251.4 10.9 %slice-start = ((s8[4718592]{0:T(1024)(128)(4,1)}), s8[4194304]{0:T(1024)(128)(4,1)S(1)}, s32[]{:S(2)}) async-start(s8[4718592]{0:T(1024)(128)(4,1)} %bitcast.259), calls=%async_computation.4 | async-start | bytes 8388608
  252.9 19.7 %copy-start.16 = (bf16[768,384]{1,0:T(8,128)(2,1)}, bf16[768,384]{1,0:T(8,128)(2,1)S(1)}, u32[]{:S(2)}) copy-start(bf16[768,384]{1,0:T(8,128)(2,1)S(1)} %get-tuple-element.255) | copy-start | bytes 1769476
  252.9 19.7 %copy-start.18 = (bf16[768,384]{1,0:T(8,128)(2,1)}, bf16[768,384]{1,0:T(8,128)(2,1)S(1)}, u32[]{:S(2)}) copy-start(bf16[768,384]{1,0:T(8,128)(2,1)S(1)} %get-tuple-element.256) | copy-start | bytes 1769476
  253.4 6.8 %copy-start.61 = (bf16[768,1536]{1,0:T(8,128)(2,1)S(1)}, bf16[768,1536]{1,0:T(8,128)(2,1)}, u32[]{:S(2)}) copy-start(bf16[768,1536]{1,0:T(8,128)(2,1)} %param.30) | copy-start | bytes 7077892
  253.4 8.9 %slice-start.1 = ((s8[4718592]{0:T(1024)(128)(4,1)}), s8[524288]{0:T(1024)(128)(4,1)S(1)}, s32[]{:S(2)}) async-start(s8[4718592]{0:T(1024)(128)(4,1)} %bitcast.259), calls=%async_computation.5 | async-start | bytes 1048576
  262.3 5.4 copy-start.3
  262.3 5.4 copy-start.43
  278.7 6.7 %collective-permute-start.8 = (bf16[768,384]{1,0:T(8,128)(2,1)S(1)}, bf16[768,384]{1,0:T(8,128)(2,1)S(1)}, u32[]{:S(2)}, u32[]{:S(2)}) collective-permute-start(bf16[768,384]{1,0:T(8,128)(2,1)S(1)} %convolution_convert_fusion.4), channel_id=1, source_target_pairs={{0,1},{1,0},{2,3},{3,2},{4,5},{5,4},{6,7},{7,6},{8,9},{9,8},{10,11... | collective-permute-start | bytes 1769480 | tf_op jit(solution)/shard_map/ppermute | solution.py:51
  281.7 181.6 %collective-permute-start.20 = (bf16[768,384]{1,0:T(8,128)(2,1)}, bf16[768,384]{1,0:T(8,128)(2,1)}, u32[]{:S(2)}, u32[]{:S(2)}) collective-permute-start(bf16[768,384]{1,0:T(8,128)(2,1)} %convolution_convert_fusion.3), channel_id=1, source_target_pairs={{0,1},{1,0},{2,3},{3,2},{4,5},{5,4},{6,7},{7,6},{8,9},{9,8},{10,11... | collective-permute-start | bytes 1769480 | tf_op jit(solution)/shard_map/ppermute | solution.py:51
  298.8 6.4 copy-start
  355.0 6.4 copy-start
  411.7 6.4 copy-start
  465.3 9.2 %collective-permute-start.21 = (bf16[2,2,2,48,384]{4,3,0,1,2:T(8,128)(2,1)S(1)}, bf16[2,2,2,48,384]{4,3,0,1,2:T(8,128)(2,1)S(1)}, u32[]{:S(2)}, u32[]{:S(2)}) collective-permute-start(bf16[2,2,2,48,384]{4,3,0,1,2:T(8,128)(2,1)S(1)} %bitcast.257), channel_id=1, source_target_pairs={{0,4},{2,6},{4,0},{6,2},{8,12},{10,14},{12,8},{14,10},{16,20},{18,... | collective-permute-start | bytes 884744 | tf_op jit(solution)/shard_map/ppermute | solution.py:51
  469.2 7.2 %copy-start.23 = (bf16[768,3,384]{0,2,1:T(8,128)(2,1)S(1)}, bf16[768,3,384]{0,2,1:T(8,128)(2,1)}, u32[]{:S(2)}) copy-start(bf16[768,3,384]{0,2,1:T(8,128)(2,1)} %copy-done.22) | copy-start | bytes 5308420
  474.6 5.2 collective-permute-start.22
  479.9 4.4 collective-permute-start.23
  481.7 5.4 copy-start.17
  481.7 5.4 copy-start.19
  481.7 5.4 copy-start.69
  481.9 19.4 %collective-permute-start.16 = (bf16[2,2,2,48,1152]{4,3,0,1,2:T(8,128)(2,1)S(1)}, bf16[2,2,2,48,1152]{4,3,0,1,2:T(8,128)(2,1)S(1)}, u32[]{:S(2)}, u32[]{:S(2)}) collective-permute-start(bf16[2,2,2,48,1152]{4,3,0,1,2:T(8,128)(2,1)S(1)} %bitcast.254), channel_id=1, source_target_pairs={{0,2},{2,0},{4,6},{6,4},{8,10},{10,8},{12,14},{14,12},{16,18},{18,... | collective-permute-start | bytes 2654216 | tf_op jit(solution)/shard_map/ppermute | solution.py:51
  483.4 19.8 %collective-permute-start.9 = (bf16[768,768]{1,0:T(8,128)(2,1)S(1)}, bf16[768,768]{1,0:T(8,128)(2,1)S(1)}, u32[]{:S(2)}, u32[]{:S(2)}) collective-permute-start(bf16[768,768]{1,0:T(8,128)(2,1)S(1)} %fusion.77), channel_id=1, source_target_pairs={{0,1},{1,0},{2,3},{3,2},{4,5},{5,4},{6,7},{7,6},{8,9},{9,8},{10,11... | collective-permute-start | bytes 3538952 | tf_op jit(solution)/shard_map/ppermute | solution.py:51
  484.4 6.6 %collective-permute-start.24 = (bf16[48,384]{1,0:T(8,128)(2,1)S(1)}, bf16[48,384]{1,0:T(8,128)(2,1)S(1)}, u32[]{:S(2)}, u32[]{:S(2)}) collective-permute-start(bf16[48,384]{1,0:T(8,128)(2,1)S(1)} %dynamic-slice_bitcast_fusion.12), channel_id=1, source_target_pairs={{0,16},{2,18},{4,20},{6,22},{8,24},{10,26},{12,28},{14,30},{16,0},... | collective-permute-start | bytes 110600 | tf_op jit(solution)/shard_map/ppermute | solution.py:51
  490.5 12.7 %copy-start.11 = (bf16[768,768]{1,0:T(8,128)(2,1)S(1)}, bf16[768,768]{1,0:T(8,128)(2,1)}, u32[]{:S(2)}) copy-start(bf16[768,768]{1,0:T(8,128)(2,1)} %copy-done.10) | copy-start | bytes 3538948
  490.5 12.7 %copy-start.34 = (f32[768]{0:T(1024)S(1)}, f32[768]{0:T(1024)}, u32[]{:S(2)}) copy-start(f32[768]{0:T(1024)} %copy-done.33) | copy-start | bytes 9220
  490.5 12.7 %copy-start.46 = (f32[768]{0:T(1024)S(1)}, f32[768]{0:T(1024)}, u32[]{:S(2)}) copy-start(f32[768]{0:T(1024)} %add_rsqrt_fusion.1) | copy-start | bytes 9220
  490.5 49.1 %collective-permute-start.30 = (bf16[768,1536]{1,0:T(8,128)(2,1)}, bf16[768,1536]{1,0:T(8,128)(2,1)}, u32[]{:S(2)}, u32[]{:S(2)}) collective-permute-start(bf16[768,1536]{1,0:T(8,128)(2,1)} %convolution_convert_fusion), channel_id=1, source_target_pairs={{0,1},{1,0},{2,3},{3,2},{4,5},{5,4},{6,7},{7,6},{8,9},{9,8},{10,11... | collective-permute-start | bytes 7077896 | tf_op jit(solution)/shard_map/ppermute | solution.py:51
  490.5 54.7 %collective-permute-start.25 = (bf16[768,1536]{1,0:T(8,128)(2,1)}, bf16[768,1536]{1,0:T(8,128)(2,1)}, u32[]{:S(2)}, u32[]{:S(2)}) collective-permute-start(bf16[768,1536]{1,0:T(8,128)(2,1)} %convolution_convert_fusion.1), channel_id=1, source_target_pairs={{0,1},{1,0},{2,3},{3,2},{4,5},{5,4},{6,7},{7,6},{8,9},{9,8},{10,11... | collective-permute-start | bytes 7077896 | tf_op jit(solution)/shard_map/ppermute | solution.py:51
  501.6 14.1 %copy-start.5 = (f32[768,768]{1,0:T(8,128)S(1)}, f32[768,768]{1,0:T(8,128)}, u32[]{:S(2)}) copy-start(f32[768,768]{1,0:T(8,128)} %copy-done.4) | copy-start | bytes 7077892
  501.6 29.2 %collective-permute-start.17 = (bf16[2,2,48,1152]{3,2,0,1:T(8,128)(2,1)S(1)}, bf16[2,2,48,1152]{3,2,0,1:T(8,128)(2,1)S(1)}, u32[]{:S(2)}, u32[]{:S(2)}) collective-permute-start(bf16[2,2,48,1152]{3,2,0,1:T(8,128)(2,1)S(1)} %dynamic-slice_bitcast_fusion.3), channel_id=1, source_target_pairs={{0,4},{2,6},{4,0},{6,2},{8,12},{10,14},{12,8},{14,10},{16,20},{18,... | collective-permute-start | bytes 1327112 | tf_op jit(solution)/shard_map/ppermute | solution.py:51
  506.0 1.3 collective-permute-start.11
  507.3 4.0 collective-permute-start.12
  511.3 3.9 collective-permute-start.13
  515.2 3.9 collective-permute-start.14
  516.9 5.7 copy-start.32
  519.1 10.5 %collective-permute-start.15 = (f32[7296]{0:T(1024)S(1)}, f32[7296]{0:T(1024)S(1)}, u32[]{:S(2)}, u32[]{:S(2)}) collective-permute-start(f32[7296]{0:T(1024)S(1)} %add.375), channel_id=1, source_target_pairs={{0,16},{2,18},{4,20},{6,22},{8,24},{10,26},{12,28},{14,30},{16,0},... | collective-permute-start | bytes 87560 | tf_op jit(solution)/shard_map/ppermute | solution.py:51
  522.7 31.3 %collective-permute-start.10 = (bf16[768,384]{1,0:T(8,128)(2,1)}, bf16[768,384]{1,0:T(8,128)(2,1)}, u32[]{:S(2)}, u32[]{:S(2)}) collective-permute-start(bf16[768,384]{1,0:T(8,128)(2,1)} %get-tuple-element.259), channel_id=1, source_target_pairs={{0,1},{1,0},{2,3},{3,2},{4,5},{5,4},{6,7},{7,6},{8,9},{9,8},{10,11... | collective-permute-start | bytes 1769480 | tf_op jit(solution)/shard_map/ppermute | solution.py:51
  529.6 10.0 %copy-start.67 = (bf16[768,1536]{1,0:T(8,128)(2,1)S(1)}, bf16[768,1536]{1,0:T(8,128)(2,1)}, u32[]{:S(2)}) copy-start(bf16[768,1536]{1,0:T(8,128)(2,1)} %copy-done.66) | copy-start | bytes 7077892
  531.0 7.9 %collective-permute-start.18 = (bf16[2,48,1152]{2,1,0:T(8,128)(2,1)S(1)}, bf16[2,48,1152]{2,1,0:T(8,128)(2,1)S(1)}, u32[]{:S(2)}, u32[]{:S(2)}) collective-permute-start(bf16[2,48,1152]{2,1,0:T(8,128)(2,1)S(1)} %dynamic-slice_bitcast_fusion.6), channel_id=1, source_target_pairs={{0,8},{2,10},{4,12},{6,14},{8,0},{10,2},{12,4},{14,6},{16,24},{18,... | collective-permute-start | bytes 663560 | tf_op jit(solution)/shard_map/ppermute | solution.py:51
  539.0 14.3 %collective-permute-start.19 = (bf16[48,1152]{1,0:T(8,128)(2,1)S(1)}, bf16[48,1152]{1,0:T(8,128)(2,1)S(1)}, u32[]{:S(2)}, u32[]{:S(2)}) collective-permute-start(bf16[48,1152]{1,0:T(8,128)(2,1)S(1)} %dynamic-slice_bitcast_fusion.10), channel_id=1, source_target_pairs={{0,16},{2,18},{4,20},{6,22},{8,24},{10,26},{12,28},{14,30},{16,0},... | collective-permute-start | bytes 331784 | tf_op jit(solution)/shard_map/ppermute | solution.py:51
  544.7 32.7 %collective-permute-start.31 = (bf16[2,2,2,48,1536]{4,3,0,1,2:T(8,128)(2,1)}, bf16[2,2,2,48,1536]{4,3,0,1,2:T(8,128)(2,1)}, u32[]{:S(2)}, u32[]{:S(2)}) collective-permute-start(bf16[2,2,2,48,1536]{4,3,0,1,2:T(8,128)(2,1)} %bitcast.191), channel_id=1, source_target_pairs={{0,4},{2,6},{4,0},{6,2},{8,12},{10,14},{12,8},{14,10},{16,20},{18,... | collective-permute-start | bytes 3538952 | tf_op jit(solution)/shard_map/ppermute | solution.py:51
  551.8 29.2 %collective-permute-start.26 = (bf16[2,2,2,48,1536]{4,3,0,1,2:T(8,128)(2,1)}, bf16[2,2,2,48,1536]{4,3,0,1,2:T(8,128)(2,1)}, u32[]{:S(2)}, u32[]{:S(2)}) collective-permute-start(bf16[2,2,2,48,1536]{4,3,0,1,2:T(8,128)(2,1)} %bitcast.192), channel_id=1, source_target_pairs={{0,2},{2,0},{4,6},{6,4},{8,10},{10,8},{12,14},{14,12},{16,18},{18,... | collective-permute-start | bytes 3538952 | tf_op jit(solution)/shard_map/ppermute | solution.py:51
  563.7 79.7 %all-to-all-start.3 = ((bf16[16,192,384]{2,1,0:T(8,128)(2,1)}), bf16[16,192,384]{2,1,0:T(8,128)(2,1)S(1)}, u32[]{:S(2)}, u32[]{:S(2)}) async-start(bf16[16,192,384]{2,1,0:T(8,128)(2,1)} %bitcast.236), calls=%async_computation.3 | async-start | bytes 4718592 | tf_op jit(solution)/shard_map/all_to_all | solution.py:159
  579.1 38.1 %collective-permute-start.32 = (bf16[2,2,48,1536]{3,2,0,1:T(8,128)(2,1)S(1)}, bf16[2,2,48,1536]{3,2,0,1:T(8,128)(2,1)S(1)}, u32[]{:S(2)}, u32[]{:S(2)}) collective-permute-start(bf16[2,2,48,1536]{3,2,0,1:T(8,128)(2,1)S(1)} %dynamic-slice_bitcast_fusion.1), channel_id=1, source_target_pairs={{0,2},{2,0},{4,6},{6,4},{8,10},{10,8},{12,14},{14,12},{16,18},{18,... | collective-permute-start | bytes 1769480 | tf_op jit(solution)/shard_map/ppermute | solution.py:51
  582.6 34.9 %collective-permute-start.27 = (bf16[2,2,48,1536]{3,2,0,1:T(8,128)(2,1)S(1)}, bf16[2,2,48,1536]{3,2,0,1:T(8,128)(2,1)S(1)}, u32[]{:S(2)}, u32[]{:S(2)}) collective-permute-start(bf16[2,2,48,1536]{3,2,0,1:T(8,128)(2,1)S(1)} %dynamic-slice_bitcast_fusion.2), channel_id=1, source_target_pairs={{0,4},{2,6},{4,0},{6,2},{8,12},{10,14},{12,8},{14,10},{16,20},{18,... | collective-permute-start | bytes 1769480 | tf_op jit(solution)/shard_map/ppermute | solution.py:51
  617.4 9.1 %collective-permute-start.33 = (bf16[2,48,1536]{2,1,0:T(8,128)(2,1)S(1)}, bf16[2,48,1536]{2,1,0:T(8,128)(2,1)S(1)}, u32[]{:S(2)}, u32[]{:S(2)}) collective-permute-start(bf16[2,48,1536]{2,1,0:T(8,128)(2,1)S(1)} %dynamic-slice_bitcast_fusion.4), channel_id=1, source_target_pairs={{0,8},{2,10},{4,12},{6,14},{8,0},{10,2},{12,4},{14,6},{16,24},{18,... | collective-permute-start | bytes 884744 | tf_op jit(solution)/shard_map/ppermute | solution.py:51
  617.7 13.6 %collective-permute-start.28 = (bf16[2,48,1536]{2,1,0:T(8,128)(2,1)S(1)}, bf16[2,48,1536]{2,1,0:T(8,128)(2,1)S(1)}, u32[]{:S(2)}, u32[]{:S(2)}) collective-permute-start(bf16[2,48,1536]{2,1,0:T(8,128)(2,1)S(1)} %dynamic-slice_bitcast_fusion.5), channel_id=1, source_target_pairs={{0,8},{2,10},{4,12},{6,14},{8,0},{10,2},{12,4},{14,6},{16,24},{18,... | collective-permute-start | bytes 884744 | tf_op jit(solution)/shard_map/ppermute | solution.py:51
  626.6 9.8 %collective-permute-start.34 = (bf16[48,1536]{1,0:T(8,128)(2,1)S(1)}, bf16[48,1536]{1,0:T(8,128)(2,1)S(1)}, u32[]{:S(2)}, u32[]{:S(2)}) collective-permute-start(bf16[48,1536]{1,0:T(8,128)(2,1)S(1)} %dynamic-slice_bitcast_fusion.7), channel_id=1, source_target_pairs={{0,16},{2,18},{4,20},{6,22},{8,24},{10,26},{12,28},{14,30},{16,0},... | collective-permute-start | bytes 442376 | tf_op jit(solution)/shard_map/ppermute | solution.py:51
  631.3 11.3 %collective-permute-start.29 = (bf16[48,1536]{1,0:T(8,128)(2,1)S(1)}, bf16[48,1536]{1,0:T(8,128)(2,1)S(1)}, u32[]{:S(2)}, u32[]{:S(2)}) collective-permute-start(bf16[48,1536]{1,0:T(8,128)(2,1)S(1)} %dynamic-slice_bitcast_fusion.8), channel_id=1, source_target_pairs={{0,16},{2,18},{4,20},{6,22},{8,24},{10,26},{12,28},{14,30},{16,0},... | collective-permute-start | bytes 442376 | tf_op jit(solution)/shard_map/ppermute | solution.py:51
  (51 other events, 138.1 us)
